TPU v7x, 128 devices: a whole 4x4x4 slice. The times are simulated.
128 devices in a mesh: win: 4 (over z_lo, core), chan: 32 (over y, z_hi, x).
Axes of the slice: x: 4, y: 4, z: 4 (z_hi: 2, z_lo: 2; z = z_hi * 2 + z_lo), core: 2. Of those that a mesh axis runs over, the one named last changes fastest.
Arguments:
- traces: bfloat16 [32, 1024, 7680], P('win', 'chan'), may hold values from -6 to 6
- filter_taps: bfloat16 [32], replicated, may hold values from 0.019897461 to 0.14941406
- good_channels: int32 [1024], P('chan'), may hold values 0 or 1
- source_index: int32 [256], replicated, may hold values from 0 to 1023, as said below
Outputs:
- correlations: float32 [256, 1024, 2048], P('win', 'chan')
Inputs may be any that keep to these rules, and one draw needn't show every extreme that they name: `source_index`: 256 distinct channel numbers; channels 0 and 1023 are among them; how many fall in one device's block varies.
All inputs are finite; a program needn't handle non-finite values. No bound on the sum of `good_channels` on one device may be relied on, other than what follows from the above.
Results may differ from a plain program's by a relative error of at most 0.0071.
Values may be sent and summed in bfloat16 or wider, within the bound.
A program may use at most 192 MiB of HBM per device.

v0:
```python
import math

import jax
import jax.numpy as jnp
from jax import lax
from jax.sharding import PartitionSpec as P

L = 7680
F = 512
LAGS = 2048
HALO = 16
SMOOTH = 64
K0 = 31


def with_halo(cells, sides, width):
    for axis, dim in sides:
        count = lax.axis_size(axis)
        ends = count - 1
        head = lax.slice_in_dim(cells, 0, width, axis=dim)
        tail = lax.slice_in_dim(cells, cells.shape[dim] - width, cells.shape[dim], axis=dim)
        cells = jnp.concatenate(
            [
                lax.ppermute(tail, axis, [(i, (i + 1) % count) for i in range(ends)]),
                cells,
                lax.ppermute(head, axis, [((i + 1) % count, i) for i in range(ends)]),
            ],
            axis=dim,
        )
    return cells


def forward_table():
    times_idx = jnp.arange(L, dtype=jnp.int32)
    band_bins = K0 + jnp.arange(F, dtype=jnp.int32)
    phase_index = times_idx[:, None] * band_bins[None, :] % L
    angles = phase_index.astype(jnp.float32) * (2.0 * math.pi / L)
    return jnp.concatenate([jnp.cos(angles), -jnp.sin(angles)], axis=1).astype(jnp.bfloat16)


def inverse_table():
    lag_values = jnp.arange(LAGS, dtype=jnp.int32) - LAGS // 2
    band_bins = K0 + jnp.arange(F, dtype=jnp.int32)
    phase_index = jnp.mod(band_bins[:, None] * lag_values[None, :], L)
    angles = phase_index.astype(jnp.float32) * (2.0 * math.pi / L)
    return jnp.concatenate([jnp.cos(angles), -jnp.sin(angles)], axis=0).astype(jnp.bfloat16)


def smoothing():
    positions = jnp.arange(F, dtype=jnp.int32)
    near = (jnp.abs(positions[:, None] - positions[None, :]) <= SMOOTH).astype(jnp.float32)
    return near / jnp.sum(near, axis=0, keepdims=True)


def whiten(spectrum):
    real_part = spectrum[..., :F]
    imag_part = spectrum[..., F:]
    magnitude = jnp.sqrt(real_part * real_part + imag_part * imag_part)
    flat = magnitude.reshape(-1, F)
    amplitude = jnp.dot(flat, smoothing(), precision=lax.Precision.HIGHEST).reshape(magnitude.shape)
    divisor = jnp.concatenate([amplitude, amplitude], axis=-1) + 1e-06
    return (spectrum / divisor).astype(jnp.bfloat16)


def make_band(filter_taps, channel_count):
    kernel = jnp.concatenate(
        [
            -filter_taps[:HALO].astype(jnp.float32),
            jnp.ones((1,), jnp.float32),
            -filter_taps[HALO:].astype(jnp.float32),
        ]
    )
    row_ids = jnp.arange(channel_count, dtype=jnp.int32)[:, None]
    columns = jnp.arange(channel_count + 2 * HALO, dtype=jnp.int32)[None, :]
    offset = columns - row_ids
    choose = offset[:, :, None] == jnp.arange(2 * HALO + 1, dtype=jnp.int32)[None, None, :]
    return jnp.sum(jnp.where(choose, kernel[None, None, :], 0.0), axis=2).astype(jnp.bfloat16)


def cross(sources, own):
    src_real = sources[..., :F]
    src_imag = sources[..., F:]
    own_real = own[..., :F]
    own_imag = own[..., F:]
    left_real = jnp.concatenate([src_real, src_imag], axis=1)
    right_real = jnp.concatenate([own_real, own_imag], axis=0)
    left_imag = jnp.concatenate([src_real, -src_imag], axis=1)
    right_imag = jnp.concatenate([own_imag, own_real], axis=0)
    real_sum = jnp.einsum("nkf,kcf->ncf", left_real, right_real, preferred_element_type=jnp.float32)
    imag_sum = jnp.einsum("nkf,kcf->ncf", left_imag, right_imag, preferred_element_type=jnp.float32)
    return jnp.concatenate([real_sum, imag_sum], axis=-1)


def per_device(traces, filter_taps, good_channels, source_index):
    window_count, channel_count, length = traces.shape
    masked = traces * good_channels.astype(jnp.bfloat16)[None, :, None]
    padded = with_halo(masked, (("chan", 1),), HALO)
    band_matrix = make_band(filter_taps, channel_count)
    keep = good_channels.astype(jnp.float32)[None, :, None]
    filtered = (
        jnp.einsum("cd,wdl->wcl", band_matrix, padded, preferred_element_type=jnp.float32) * keep
    ).astype(jnp.bfloat16)
    spectrum = jnp.einsum(
        "wcl,lf->wcf", filtered, forward_table(), preferred_element_type=jnp.float32
    )
    whitened = whiten(spectrum)
    everything = lax.all_gather(whitened, "chan", axis=1, tiled=True)
    channel_ids = jnp.arange(everything.shape[1], dtype=jnp.int32)
    selector = (source_index[:, None] == channel_ids[None, :]).astype(jnp.bfloat16)
    picked = jnp.einsum(
        "sc,wcf->swf", selector, everything, preferred_element_type=jnp.float32
    ).astype(jnp.bfloat16)
    group_count = lax.axis_size("win")
    stacked = lax.psum_scatter(cross(picked, whitened), "win", scatter_dimension=0, tiled=True)
    stacked_rounded = stacked.astype(jnp.bfloat16)
    source_rows = stacked_rounded.shape[0]
    flat = stacked_rounded.reshape(source_rows * channel_count, 2 * F)
    scaling = 1.0 / math.sqrt(F * window_count * group_count)
    lagged = jnp.dot(flat, inverse_table(), preferred_element_type=jnp.float32) * scaling
    return lagged.reshape(source_rows, channel_count, LAGS)


def solution(mesh):
    placed = (P("win", "chan", None), P(), P("chan"), P())
    return jax.shard_map(
        per_device, mesh=mesh, in_specs=placed, out_specs=P("win", "chan", None), check_vma=False
    )
```

profile of v0, /device:TPU:4, one launch (start us, length us, event | category | flops | bytes accessed | tf_op | source)
XLA Modules:
  0.0 656.6 jit_solution(1740124001375795375)
XLA Ops:
  6.5 0.7 fusion.47
  7.3 2.4 broadcast_multiply_fusion
  9.7 0.3 fusion.45
  10.0 3.1 collective-permute-start
  13.1 2.7 collective-permute-start.1
  15.9 0.1 convert_reduce_fusion
  16.1 0.1 pad_maximum_fusion.5
  16.2 0.1 select_reduce_fusion
  16.3 66.9 %cosine_convert_fusion = (bf16[7680,512]{1,0:T(8,128)(2,1)}, bf16[7680,512]{1,0:T(8,128)(2,1)}) fusion(s32[512]{0:T(512)S(1)} %iota_add_fusion.1), kind=kLoop, calls=%fused_computation.6 | loop fusion | flops 47185920 | bytes 15730688 | tf_op jit(solution)/shard_map/convert.2
  83.3 1.4 copy-done.4
  84.6 10.6 %fusion.4 = f32[8,32,1024]{2,1,0:T(8,128)S(1)} fusion(bf16[7680,512]{1,0:T(8,128)(2,1)} %get-tuple-element.19, bf16[7680,512]{1,0:T(8,128)(2,1)} %get-tuple-element.18, bf16[8,16,7680]{2,1,0:T(8,128)(2,1)} %copy-done.4, bf16[8,32,7680]{2,1,0:T(8,128)(2,1)} %copy-done.1, bf16[8,16,7680]{2,1,0:T(8,128)(2,1)S(1)} %collective-permute-done, ...), kind=kOutput, calls=%fused_computation.10 | convolution fusion | flops 4337172480 | bytes 24645760 | tf_op jit(solution)/shard_map/wcl,lf->wcf/dot_general | solution.py:103
  95.3 1.2 fusion.24
  96.5 1.0 fusion.27
  97.5 0.2 reduce-scatter.2.cloned.1.call-start
  97.8 1.1 fusion.46
  98.8 0.1 pad_maximum_fusion.3
  98.9 2.0 copy.19
  100.9 2.8 copy.21
  103.8 154.7 %all-gather.2.cloned.1.call-done = bf16[8,1024,1024]{2,1,0:T(8,128)(2,1)} async-done(((bf16[8,32,1024]{2,1,0:T(8,128)(2,1)}), bf16[8,1024,1024]{2,1,0:T(8,128)(2,1)}) %all-gather.2.cloned.1.call-update) | async-done | bytes 16777232 | tf_op jit(solution)/shard_map/all_gather | solution.py:107
  258.5 10.5 %convolution_convert_fusion = bf16[256,8,1024]{2,0,1:T(8,128)(2,1)S(1)} fusion(bf16[8,1024,1024]{2,1,0:T(8,128)(2,1)} %all-gather.2.cloned.1.call-done, s32[256]{0:T(256)S(1)} %copy-done.5), kind=kOutput, calls=%fused_computation.37 | convolution fusion | flops 4297326592 | bytes 20972544 | tf_op jit(solution)/shard_map/sc,wcf->swf/dot_general | solution.py:110
  269.0 0.4 fusion.44
  269.4 3.7 pad_maximum_fusion.2
  273.1 7.9 %copy.20 = bf16[256,16,512]{0,1,2:T(8,128)(2,1)} copy(bf16[256,16,512]{2,0,1:T(8,128)(2,1)} %get-tuple-element.10) | data formatting | bytes 8388608 | tf_op jit(solution)/shard_map/concatenate | solution.py:85
  281.0 7.8 %copy.22 = bf16[256,16,512]{0,1,2:T(8,128)(2,1)} copy(bf16[256,16,512]{2,0,1:T(8,128)(2,1)} %get-tuple-element.11) | data formatting | bytes 8388608 | tf_op jit(solution)/shard_map/concatenate | solution.py:87
  288.9 4.4 convolution_bitcast_fusion.1
  293.3 10.1 %convolution_bitcast_fusion = f32[256,32,512]{0,1,2:T(8,128)} fusion(bf16[16,32,512]{1,0,2:T(8,128)(2,1)} %copy.21, bf16[256,16,512]{0,1,2:T(8,128)(2,1)S(1)} %copy-done), kind=kOutput, calls=%fused_computation.16 | convolution fusion | flops 134217728 | bytes 21495808 | tf_op jit(solution)/shard_map/nkf,kcf->ncf/dot_general | solution.py:90
  303.4 19.0 %pad_maximum_fusion = f32[256,32,1024]{0,1,2:T(8,128)} fusion(f32[256,32,512]{0,1,2:T(8,128)} %convolution_bitcast_fusion, f32[256,32,512]{0,1,2:T(8,128)S(1)} %convolution_bitcast_fusion.1), kind=kLoop, calls=%fused_computation | loop fusion | flops 8388608 | bytes 67108864 | tf_op jit(solution)/shard_map/concatenate | solution.py:91
  322.4 32.3 %copy.23 = f32[256,32,1024]{2,1,0:T(8,128)} copy(f32[256,32,1024]{0,1,2:T(8,128)} %pad_maximum_fusion) | data formatting | bytes 67108864 | tf_op jit(solution)/shard_map/concatenate | solution.py:91
  354.7 18.7 %cosine_convert_fusion.1 = (bf16[512,2048]{1,0:T(8,128)(2,1)S(1)}, bf16[512,2048]{1,0:T(8,128)(2,1)}) fusion(s32[2048]{0:T(1024)S(1)} %iota_add_fusion, s32[512]{0:T(512)S(1)} %iota_add_fusion.1), kind=kLoop, calls=%fused_computation.32 | loop fusion | flops 12582912 | bytes 4204544 | tf_op jit(solution)/shard_map/convert
  373.4 260.3 %reduce-scatter.2.cloned.1.call-done = f32[64,32,1024]{2,1,0:T(8,128)} async-done(((f32[256,32,1024]{2,1,0:T(8,128)}), f32[64,32,1024]{2,1,0:T(8,128)}) %reduce-scatter.2.cloned.1.call-update) | async-done | bytes 8388624 | tf_op jit(solution)/shard_map/reduce_scatter | solution.py:114
  633.7 4.2 convert_element_type.59
  637.9 11.8 %convolution_multiply_fusion.1 = f32[2048,2048]{1,0:T(8,128)} fusion(bf16[2048,1024]{1,0:T(8,128)(2,1)S(1)} %bitcast.29, bf16[512,2048]{1,0:T(8,128)(2,1)S(1)} %copy-done.2, bf16[512,2048]{1,0:T(8,128)(2,1)S(1)} %get-tuple-element.16), kind=kOutput, calls=%fused_computation.15 | convolution fusion | flops 8602517504 | bytes 25165824 | tf_op jit(solution)/shard_map/dot_general | solution.py:119
  (20 shorter events, 0.2 us)
Async XLA Ops:
  6.5 251.9 %all-gather.2.cloned.1.call-start = ((), (), s32[]{:S(2)}) async-start(), calls=%async_computation.1 | async-start | bytes 17301504 | tf_op jit(solution)/shard_map/all_gather | solution.py:107
  9.7 73.5 %copy-start.1 = (bf16[8,32,7680]{2,1,0:T(8,128)(2,1)}, bf16[8,32,7680]{2,1,0:T(8,128)(2,1)S(1)}, u32[]{:S(2)}) copy-start(bf16[8,32,7680]{2,1,0:T(8,128)(2,1)S(1)} %broadcast_multiply_fusion) | copy-start | bytes 11796484
  9.7 6.3 copy-start.3
  10.0 73.2 %collective-permute-start = (bf16[8,16,7680]{2,1,0:T(8,128)(2,1)S(1)}, bf16[8,16,7680]{2,1,0:T(8,128)(2,1)S(1)}, u32[]{:S(2)}, u32[]{:S(2)}) collective-permute-start(bf16[8,16,7680]{2,1,0:T(8,128)(2,1)S(1)} %get-tuple-element.8), channel_id=1, source_target_pairs={{0,1},{1,2},{2,3},{3,4},{4,5},{5,6},{6,7},{7,8},{8,9},{9,10},{10,1... | collective-permute-start | bytes 5898248 | tf_op jit(solution)/shard_map/ppermute | solution.py:24
  13.1 70.1 %collective-permute-start.1 = (bf16[8,16,7680]{2,1,0:T(8,128)(2,1)S(1)}, bf16[8,16,7680]{2,1,0:T(8,128)(2,1)S(1)}, u32[]{:S(2)}, u32[]{:S(2)}) collective-permute-start(bf16[8,16,7680]{2,1,0:T(8,128)(2,1)S(1)} %get-tuple-element.9), channel_id=1, source_target_pairs={{1,0},{2,1},{3,2},{4,3},{5,4},{6,5},{7,6},{8,7},{9,8},{10,9},{11,1... | collective-permute-start | bytes 5898248 | tf_op jit(solution)/shard_map/ppermute | solution.py:26
  83.2 1.4 copy-start.4
  97.5 160.9 %copy-start.5 = (s32[256]{0:T(256)S(1)}, s32[256]{0:T(256)}, u32[]{:S(2)}) copy-start(s32[256]{0:T(256)} %param.7) | copy-start | bytes 3076
  97.5 536.2 %reduce-scatter.2.cloned.1.call-start = ((), (), s32[]{:S(2)}) async-start(), calls=%async_computation.2 | async-start | bytes 41943040 | tf_op jit(solution)/shard_map/reduce_scatter | solution.py:114
  288.9 4.4 copy-start
  633.7 4.2 copy-start.2
Sparse Core Ops, SparseCore 0:
  97.7 160.7 all-gather.1
  354.8 278.8 reduce-scatter.1
where the time goes:
time: 659 us; the launch traced here: 657 us
  waiting for transfers between devices  415 us (63%)
  other arithmetic  118 us (18%)
  local copies, waits for them, and re-layouts  55.6 us (8%)
  matrix products  48.7 us (7%)
  between operations  13.6 us (2%)
    reduce_scatter x1, waiting for transfers between devices, per_device(): lax.psum_scatter(cross(picked, whitened), 'win', scatter_dimension=0, til...  260 us
    all_gather x1, waiting for transfers between devices, per_device(): everything = lax.all_gather(whitened, 'chan', axis=1, tiled=True)  155 us
    another operation x2, other arithmetic  85.7 us
    concatenate x1, local copies, waits for them, and re-layouts, cross(): return jnp.concatenate([real_sum, imag_sum], axis=-1)  32.3 us
    concatenate x1, other arithmetic, cross(): return jnp.concatenate([real_sum, imag_sum], axis=-1)  19 us
  transfers between devices with their start and end apart: 4, of which 2 were waited for; matrix products, arithmetic and copies ran while one was open for 14% of the time, Pallas kernels for 0%

commit v1 on v0

v1 whole, which is shorter than its diff:
```python
import math

import jax
import jax.numpy as jnp
from jax import lax
from jax.sharding import PartitionSpec as P

L = 7680
F = 512
LAGS = 2048
HALO = 16
SMOOTH = 64
K0 = 31


def turn(bins, steps):
    phase = jnp.mod(bins * steps, L).astype(jnp.float32) * (2.0 * math.pi / L)
    return jnp.cos(phase), jnp.sin(phase)


def forward_table():
    bins = K0 + jnp.arange(F, dtype=jnp.int32)
    step = 64
    ca, sa = turn(bins[None, :], step * jnp.arange(L // step, dtype=jnp.int32)[:, None])
    cb, sb = turn(bins[None, :], jnp.arange(step, dtype=jnp.int32)[:, None])
    ca, sa, cb, sb = lax.optimization_barrier((ca, sa, cb, sb))
    cosine = ca[:, None] * cb[None] - sa[:, None] * sb[None]
    sine = sa[:, None] * cb[None] + ca[:, None] * sb[None]
    return (
        cosine.reshape(L, F).astype(jnp.bfloat16),
        (-sine).reshape(L, F).astype(jnp.bfloat16),
    )


def inverse_table():
    bins = (K0 + jnp.arange(F, dtype=jnp.int32))[:, None]
    step = 128
    ca, sa = turn(bins, step * jnp.arange(LAGS // step, dtype=jnp.int32)[None, :] - LAGS // 2)
    cb, sb = turn(bins, jnp.arange(step, dtype=jnp.int32)[None, :])
    ca, sa, cb, sb = lax.optimization_barrier((ca, sa, cb, sb))
    cosine = ca[:, :, None] * cb[:, None] - sa[:, :, None] * sb[:, None]
    sine = sa[:, :, None] * cb[:, None] + ca[:, :, None] * sb[:, None]
    return (
        cosine.reshape(F, LAGS).astype(jnp.bfloat16),
        (-sine).reshape(F, LAGS).astype(jnp.bfloat16),
    )


def smoothing():
    positions = jnp.arange(F, dtype=jnp.int32)
    near = (jnp.abs(positions[:, None] - positions[None, :]) <= SMOOTH).astype(jnp.float32)
    return near / jnp.sum(near, axis=0, keepdims=True)


def make_band(filter_taps, channel_count):
    kernel = jnp.concatenate(
        [
            -filter_taps[:HALO].astype(jnp.float32),
            jnp.ones((1,), jnp.float32),
            -filter_taps[HALO:].astype(jnp.float32),
        ]
    )
    row_ids = jnp.arange(channel_count, dtype=jnp.int32)[:, None]
    columns = jnp.arange(channel_count + 2 * HALO, dtype=jnp.int32)[None, :]
    offset = columns - row_ids
    choose = offset[:, :, None] == jnp.arange(2 * HALO + 1, dtype=jnp.int32)[None, None, :]
    return jnp.sum(jnp.where(choose, kernel[None, None, :], 0.0), axis=2)


def with_halo(cells, axis, dim, width):
    count = lax.axis_size(axis)
    ends = count - 1
    head = lax.slice_in_dim(cells, 0, width, axis=dim)
    tail = lax.slice_in_dim(cells, cells.shape[dim] - width, cells.shape[dim], axis=dim)
    before = lax.ppermute(tail, axis, [(i, (i + 1) % count) for i in range(ends)])
    after = lax.ppermute(head, axis, [((i + 1) % count, i) for i in range(ends)])
    return jnp.concatenate([before, cells, after], axis=dim)


def per_device(traces, filter_taps, good_channels, source_index):
    windows, channels, length = traces.shape
    groups, blocks = lax.axis_size("win"), lax.axis_size("chan")
    sources = source_index.shape[0]
    bins = F // blocks
    everyone = channels * blocks
    good = good_channels.astype(jnp.float32)[None, :, None]

    rows = traces.reshape(windows * channels, length)
    cosine, sine = forward_table()
    dot = lambda a, b: jnp.dot(a, b, preferred_element_type=jnp.float32)
    spectrum = jnp.stack([dot(rows, cosine), dot(rows, sine)], axis=1)
    spectrum = spectrum.reshape(windows, channels, 2 * F) * good
    padded = with_halo(spectrum, "chan", 1, HALO)
    band = make_band(filter_taps, channels)
    filtered = jnp.einsum("cd,wdf->wcf", band, padded, precision=lax.Precision.HIGHEST) * good

    real, imag = filtered[..., :F], filtered[..., F:]
    magnitude = jnp.sqrt(real * real + imag * imag).reshape(-1, F)
    amplitude = jnp.dot(magnitude, smoothing(), precision=lax.Precision.HIGHEST)
    divisor = amplitude.reshape(real.shape) + 1e-06
    whitened = jnp.stack([real / divisor, imag / divisor], axis=2).astype(jnp.bfloat16)

    split = whitened.reshape(windows, channels, 2, blocks, bins)
    split = jnp.transpose(split, (3, 4, 2, 0, 1)).reshape(blocks, bins * 2, windows * channels)
    mixed = lax.all_to_all(split, "chan", 0, 0, tiled=True)
    mixed = mixed.reshape(blocks, bins * 2 * windows, channels)
    mixed = jnp.transpose(mixed, (1, 0, 2)).reshape(bins * 2 * windows, everyone)
    ids = jnp.arange(everyone, dtype=jnp.int32)
    selector = (ids[:, None] == source_index[None, :]).astype(jnp.bfloat16)
    picked = dot(mixed, selector).astype(jnp.bfloat16)
    share = sources // groups
    picked = picked.reshape(bins * 2 * windows, groups, share)
    picked = jnp.transpose(picked, (1, 0, 2))
    picked = lax.all_to_all(picked, "win", 0, 0, tiled=True)
    picked = picked.reshape(groups, bins, 2, windows, share)
    picked = jnp.transpose(picked, (1, 2, 0, 3, 4)).reshape(bins, groups * windows, 2 * share)
    gathered = lax.all_gather(picked, "chan", axis=0, tiled=True)
    gathered = gathered.reshape(F, 2 * groups * windows, share)

    own = lax.all_gather(whitened, "win", axis=0, tiled=True)
    own = jnp.transpose(own, (3, 2, 0, 1))
    own_real, own_imag = own[:, 0], own[:, 1]
    left = jnp.concatenate([own_real, own_imag], axis=1)
    right = jnp.concatenate([own_imag, -own_real], axis=1)
    both = jnp.concatenate([left, right], axis=2)
    stacked = jnp.einsum("fks,fkc->fsc", gathered, both, preferred_element_type=jnp.float32)
    stacked = stacked.astype(jnp.bfloat16).reshape(F, share, 2, channels)
    stacked = jnp.transpose(stacked, (1, 3, 2, 0)).reshape(share * channels, 2, F)
    scaling = 1.0 / math.sqrt(F * windows * groups)
    cosine, sine = inverse_table()
    lagged = (dot(stacked[:, 0], cosine) + dot(stacked[:, 1], sine)) * scaling
    return lagged.reshape(share, channels, LAGS)


def solution(mesh):
    placed = (P("win", "chan", None), P(), P("chan"), P())
    return jax.shard_map(
        per_device, mesh=mesh, in_specs=placed, out_specs=P("win", "chan", None), check_vma=False
    )
```

time: 659 us -> 246 us (0.37)
  waiting for transfers between devices: 415 us -> 72.7 us
  other arithmetic: 118 us -> 19.5 us
  blocking collectives: 0 us -> 31.9 us
  matrix products: 48.7 us -> 39.6 us
    reduce_scatter x1 -> x0, waiting for transfers between devices: 260 us -> none  [per_device(): lax.psum_scatter(cross(picked, whitened), 'win', scatter_dimension=0, til...]
    all_gather x1 -> x2, waiting for transfers between devices: 155 us -> 58.5 us  [the longest x1 58.5 us: per_device(): gathered = lax.all_gather(picked, 'chan', axis=0, tiled=True)]
    another operation x2, other arithmetic: 85.7 us -> 0.91 us  [the longest x1 0.84 us: per_device(): jnp.stack([real / divisor, imag / divisor], axis=2).astype(jnp.bfloat16)]
    concatenate x5 -> x1, local copies, waits for them, and re-layouts: 52.8 us -> 13 us  [per_device(): both = jnp.concatenate([left, right], axis=2)]
    all_to_all x0 -> x2, blocking collectives: none -> 31.9 us  [the longest x1 22.5 us: per_device(): mixed = lax.all_to_all(split, 'chan', 0, 0, tiled=True)]
    concatenate x3 -> x1, other arithmetic: 22.8 us -> 2.23 us  [per_device(): both = jnp.concatenate([left, right], axis=2)]
    reshape x0 -> x5, local copies, waits for them, and re-layouts: none -> 19.7 us  [the longest x1 15.6 us: per_device(): gathered = gathered.reshape(F, 2 * groups * windows, share)]
    convert_element_type x0 -> x1, local copies, waits for them, and re-layouts: none -> 9.74 us  [per_device(): stacked = stacked.astype(jnp.bfloat16).reshape(F, share, 2, channels)]
  transfers between devices with their start and end apart: 4 -> 4, of which waited for: 2 -> 3; matrix products, arithmetic and copies ran while one was open for 14% -> 14% of each run, Pallas kernels for 0% -> 0%
where the time goes in v1:
time: 246 us; the launch traced here: 243 us
  waiting for transfers between devices  72.7 us (30%)
  local copies, waits for them, and re-layouts  59.7 us (24%)
  matrix products  39.6 us (16%)
  blocking collectives  31.9 us (13%)
  other arithmetic  19.5 us (8%)
  between operations  13.7 us (6%)
  starting transfers between devices  6.07 us (2%)
    all_gather x1, waiting for transfers between devices, per_device(): gathered = lax.all_gather(picked, 'chan', axis=0, tiled=True)  58.5 us
    dot_general x5, matrix products, per_device(): dot = lambda a, b: jnp.dot(a, b, preferred_element_type=jnp.float32)  25.7 us
    all_to_all x1, blocking collectives, per_device(): mixed = lax.all_to_all(split, 'chan', 0, 0, tiled=True)  22.5 us
    reshape x1, local copies, waits for them, and re-layouts, per_device(): gathered = gathered.reshape(F, 2 * groups * windows, share)  15.6 us
    concatenate x1, local copies, waits for them, and re-layouts, per_device(): both = jnp.concatenate([left, right], axis=2)  13 us
    dot_general x1, matrix products, per_device(): jnp.einsum('fks,fkc->fsc', gathered, both, preferred_element_type=jnp.flo...  11.3 us
    convert_element_type x1, local copies, waits for them, and re-layouts, per_device(): stacked = stacked.astype(jnp.bfloat16).reshape(F, share, 2, channels)  9.74 us
    all_to_all x1, blocking collectives, per_device(): picked = lax.all_to_all(picked, 'win', 0, 0, tiled=True)  9.42 us
  transfers between devices with their start and end apart: 4, of which 3 were waited for; matrix products, arithmetic and copies ran while one was open for 14% of the time, Pallas kernels for 0%

profile of v1, /device:TPU:4, one launch (start us, length us, event | category | flops | bytes accessed | tf_op | source)
XLA Modules:
  0.0 243.2 jit_solution(9256046249764488601)
XLA Ops:
  7.1 1.1 fusion.46
  8.2 4.6 %subtract_convert_fusion = (bf16[120,64,512]{2,1,0:T(8,128)(2,1)S(1)}, bf16[120,64,512]{2,1,0:T(8,128)(2,1)S(1)}) fusion(f32[64,512]{1,0:T(8,128)S(1)} %get-tuple-element.16, f32[120,512]{1,0:T(8,128)S(1)} %get-tuple-element.15, f32[64,512]{1,0:T(8,128)S(1)} %get-tuple-element.14, f32[120,512]{1,0:T(8,128)S(1)} %get-tuple-element.13), kind=kLoop, calls=%fused_computation.2 | loop fusion | flops 35389440 | bytes 16482304 | tf_op jit(solution)/shard_map/convert_element_type | solution.py:30
  12.8 2.2 convolution_bitcast_fusion
  15.1 2.2 convolution_bitcast_fusion.1
  18.0 0.9 reshape.176
  19.2 3.1 %collective-permute-start = (f32[8,16,1024]{2,1,0:T(8,128)S(1)}, f32[8,16,1024]{2,1,0:T(8,128)S(1)}, u32[]{:S(2)}, u32[]{:S(2)}) collective-permute-start(f32[8,16,1024]{2,1,0:T(8,128)S(1)} %get-tuple-element.27), channel_id=1, source_target_pairs={{0,1},{1,2},{2,3},{3,4},{4,5},{5,6},{6,7},{7,8},{8,9},{9,10},{10,1... | collective-permute-start | bytes 1572872 | tf_op jit(solution)/shard_map/ppermute | solution.py:75
  22.3 2.7 %collective-permute-start.1 = (f32[8,16,1024]{2,1,0:T(8,128)S(1)}, f32[8,16,1024]{2,1,0:T(8,128)S(1)}, u32[]{:S(2)}, u32[]{:S(2)}) collective-permute-start(f32[8,16,1024]{2,1,0:T(8,128)S(1)} %get-tuple-element.28), channel_id=1, source_target_pairs={{1,0},{2,1},{3,2},{4,3},{5,4},{6,5},{7,6},{8,7},{9,8},{10,9},{11,1... | collective-permute-start | bytes 1572872 | tf_op jit(solution)/shard_map/ppermute | solution.py:76
  25.5 9.3 %collective-permute-done = f32[8,16,1024]{2,1,0:T(8,128)S(1)} collective-permute-done((f32[8,16,1024]{2,1,0:T(8,128)S(1)}, f32[8,16,1024]{2,1,0:T(8,128)S(1)}, u32[]{:S(2)}, u32[]{:S(2)}) %collective-permute-start) | collective-permute-done | bytes 524320 | tf_op jit(solution)/shard_map/ppermute | solution.py:75
  34.8 4.9 %collective-permute-done.1 = f32[8,16,1024]{2,1,0:T(8,128)S(1)} collective-permute-done((f32[8,16,1024]{2,1,0:T(8,128)S(1)}, f32[8,16,1024]{2,1,0:T(8,128)S(1)}, u32[]{:S(2)}, u32[]{:S(2)}) %collective-permute-start.1) | collective-permute-done | bytes 524320 | tf_op jit(solution)/shard_map/ppermute | solution.py:76
  39.7 1.2 fusion.14
  40.9 1.3 divide_convert_fusion.1
  42.2 0.8 pad_maximum_fusion.1
  44.8 2.4 %copy.34 = bf16[32,16,2,8,32]{4,3,2,1,0:T(8,128)(2,1)S(1)} copy(bf16[32,16,2,8,32]{4,1,0,3,2:T(8,128)(2,1)S(1)} %maximum_bitcast_fusion) | data formatting | bytes 1048576 | tf_op jit(solution)/shard_map/transpose | solution.py:104
  47.2 1.5 reshape.177
  48.7 22.5 %all_to_all.10 = bf16[32,32,256]{2,1,0:T(8,128)(2,1)S(1)} all-to-all(bf16[32,32,256]{2,1,0:T(8,128)(2,1)S(1)} %reshape.177), channel_id=1, replica_groups=mesh['win'=4,'chan'=32] {'chan'}, dimensions={0} | all-to-all | bytes 1048576 | tf_op jit(solution)/shard_map/all_to_all | solution.py:105
  71.1 0.9 reshape.178
  73.4 9.4 %all_to_all.11 = bf16[4,256,64]{1,2,0:T(8,128)(2,1)S(1)} all-to-all(bf16[4,256,64]{1,2,0:T(8,128)(2,1)S(1)} %bitcast.90), channel_id=1, replica_groups=mesh['win'=4,'chan'=32] {'win'}, dimensions={0} | all-to-all | bytes 262144 | tf_op jit(solution)/shard_map/all_to_all | solution.py:114
  83.9 1.1 fusion.34
  85.0 1.1 fusion.38
  86.1 5.5 %negate_convert_fusion.1 = (bf16[512,16,128]{2,1,0:T(8,128)(2,1)S(1)}, bf16[512,16,128]{2,1,0:T(8,128)(2,1)}) fusion(f32[512,128]{1,0:T(8,128)S(1)} %get-tuple-element.20, f32[512,16]{1,0:T(8,128)S(1)} %get-tuple-element.19, f32[512,128]{1,0:T(8,128)S(1)} %get-tuple-element.18, f32[512,16]{1,0:T(8,128)S(1)} %get-tuple-element.17), kind=kLoop, calls=%fused_computation.5 | loop fusion | flops 9437184 | bytes 4784128 | tf_op jit(solution)/shard_map/convert_element_type | solution.py:45
  91.7 1.3 fusion.59
  93.0 1.8 slice_bitcast_fusion.5
  94.7 2.2 maximum_maximum_fusion
  97.0 13.0 %copy.40 = bf16[512,64,64]{2,1,0:T(8,128)(2,1)} copy(bf16[512,64,64]{0,2,1:T(8,128)(2,1)} %maximum_maximum_fusion) | data formatting | bytes 8388608 | tf_op jit(solution)/shard_map/concatenate | solution.py:125
  110.0 58.5 %all-gather.3.cloned.1.call-done = bf16[512,32,128]{2,1,0:T(8,128)(2,1)} async-done(((bf16[16,32,128]{2,1,0:T(8,128)(2,1)}), bf16[512,32,128]{2,1,0:T(8,128)(2,1)}) %all-gather.3.cloned.1.call-update) | async-done | bytes 4194320 | tf_op jit(solution)/shard_map/all_gather | solution.py:117
  168.5 7.6 %copy.38 = bf16[512,32,128]{0,2,1:T(8,128)(2,1)} copy(bf16[512,32,128]{2,1,0:T(8,128)(2,1)} %all-gather.3.cloned.1.call-done) | data formatting | bytes 8388608 | tf_op jit(solution)/shard_map/all_gather | solution.py:117
  176.1 15.6 %copy.39 = bf16[512,64,64]{1,2,0:T(8,128)(2,1)} copy(bf16[512,64,64]{0,2,1:T(8,128)(2,1)} %bitcast.73) | data formatting | bytes 8388608 | tf_op jit(solution)/shard_map/reshape | solution.py:118
  191.7 11.3 %convolution_convert_fusion = bf16[512,64,64]{2,1,0:T(8,128)(2,1)} fusion(bf16[512,64,64]{1,2,0:T(8,128)(2,1)} %copy.39, bf16[512,64,64]{2,1,0:T(8,128)(2,1)} %copy.40), kind=kOutput, calls=%fused_computation.3 | convolution fusion | flops 270532608 | bytes 12582912 | tf_op jit(solution)/shard_map/fks,fkc->fsc/dot_general | solution.py:126
  203.0 9.7 %copy.41 = bf16[512,64,64]{0,2,1:T(8,128)(2,1)} copy(bf16[512,64,64]{2,1,0:T(8,128)(2,1)} %convolution_convert_fusion) | data formatting | bytes 8388608 | tf_op jit(solution)/shard_map/convert_element_type | solution.py:127
  212.8 2.7 %copy.42 = bf16[64,32,2,512]{3,1,0,2:T(8,128)(2,1)S(1)} copy(bf16[64,32,2,512]{3,1,2,0:T(8,128)(2,1)} %bitcast.74) | data formatting | bytes 8388608 | tf_op jit(solution)/shard_map/transpose | solution.py:128
  215.6 8.7 %fusion.2 = f32[2048,2048]{1,0:T(8,128)} fusion(bf16[64,8,16,128]{3,2,1,0:T(8,128)(2,1)S(1)} %bitcast.85, bf16[2048,2,512]{2,0,1:T(8,128)(2,1)S(1)} %bitcast.75), kind=kOutput, calls=%fused_computation.9 | convolution fusion | flops 4294967296 | bytes 20971520 | tf_op jit(solution)/shard_map/dot_general | solution.py:90
  224.3 12.0 %add_multiply_fusion = f32[2048,2048]{1,0:T(8,128)} fusion(f32[2048,2048]{1,0:T(8,128)} %fusion.2, bf16[64,8,16,128]{3,2,1,0:T(8,128)(2,1)S(1)} %bitcast.77, bf16[2048,2,512]{2,0,1:T(8,128)(2,1)S(1)} %bitcast.76), kind=kOutput, calls=%fused_computation | convolution fusion | flops 4303355904 | bytes 37748736 | tf_op jit(solution)/shard_map/dot_general | solution.py:90
  (37 shorter events, 6.2 us)
Async XLA Ops:
  6.5 85.1 %all-gather.5.cloned.1.call-start = ((), (), s32[]{:S(2)}) async-start(), calls=%async_computation.3 | async-start | bytes 2621440 | tf_op jit(solution)/shard_map/all_gather | solution.py:120
  8.2 4.7 %copy-start.2 = (bf16[8,32,7680]{2,1,0:T(8,128)(2,1)S(1)}, bf16[8,32,7680]{2,1,0:T(8,128)(2,1)}, u32[]{:S(2)}) copy-start(bf16[8,32,7680]{2,1,0:T(8,128)(2,1)} %param.4) | copy-start | bytes 11796484
  17.3 1.6 copy-start.4
  17.4 7.8 %copy-start.1 = (bf16[32]{0:T(256)(128)(2,1)S(1)}, bf16[32]{0:T(256)(128)(2,1)}, u32[]{:S(2)}) copy-start(bf16[32]{0:T(256)(128)(2,1)} %param.5) | copy-start | bytes 196
  19.2 15.6 %collective-permute-start = (f32[8,16,1024]{2,1,0:T(8,128)S(1)}, f32[8,16,1024]{2,1,0:T(8,128)S(1)}, u32[]{:S(2)}, u32[]{:S(2)}) collective-permute-start(f32[8,16,1024]{2,1,0:T(8,128)S(1)} %get-tuple-element.27), channel_id=1, source_target_pairs={{0,1},{1,2},{2,3},{3,4},{4,5},{5,6},{6,7},{7,8},{8,9},{9,10},{10,1... | collective-permute-start | bytes 1572872 | tf_op jit(solution)/shard_map/ppermute | solution.py:75
  22.3 17.3 %collective-permute-start.1 = (f32[8,16,1024]{2,1,0:T(8,128)S(1)}, f32[8,16,1024]{2,1,0:T(8,128)S(1)}, u32[]{:S(2)}, u32[]{:S(2)}) collective-permute-start(f32[8,16,1024]{2,1,0:T(8,128)S(1)} %get-tuple-element.28), channel_id=1, source_target_pairs={{1,0},{2,1},{3,2},{4,3},{5,4},{6,5},{7,6},{8,7},{9,8},{10,9},{11,1... | collective-permute-start | bytes 1572872 | tf_op jit(solution)/shard_map/ppermute | solution.py:76
  43.1 125.4 %all-gather.3.cloned.1.call-start = ((), (), s32[]{:S(2)}) async-start(), calls=%async_computation.2 | async-start | bytes 4325376 | tf_op jit(solution)/shard_map/all_gather | solution.py:117
  47.2 25.6 %copy-start.3 = (s32[256]{0:T(256)S(1)}, s32[256]{0:T(256)}, u32[]{:S(2)}) copy-start(s32[256]{0:T(256)} %param.7) | copy-start | bytes 3076
  212.8 2.9 %copy-start = (bf16[512,16,128]{2,1,0:T(8,128)(2,1)S(1)}, bf16[512,16,128]{2,1,0:T(8,128)(2,1)}, u32[]{:S(2)}) copy-start(bf16[512,16,128]{2,1,0:T(8,128)(2,1)} %get-tuple-element.26) | copy-start | bytes 6291460
Sparse Core Ops, SparseCore 0:
  43.2 40.3 all-gather.4
  86.6 81.9 all-gather.2

commit v2 on v0

v2 whole, which is shorter than its diff:
```python
import functools
import math

import jax
import jax.numpy as jnp
from jax import lax
from jax.experimental import pallas as pl
from jax.experimental.pallas import tpu as pltpu
from jax.sharding import PartitionSpec as P

L = 7680
F = 512
LAGS = 2048
HALO = 16
SMOOTH = 64
K0 = 31

WIN = 4
BLK = 32
NX = 4
NZ = 2
NY = 4
W = 8
C = 32
S = 64
BINS = F // BLK
QUADS = F // 4
PACK = 4
DEEP = 2 * W * WIN
MESH = pl.DeviceIdType.MESH
f32, bf16, i32 = jnp.float32, jnp.bfloat16, jnp.int32


def iota(shape, dim):
    return lax.broadcasted_iota(i32, shape, dim)


def mxu(a, b):
    return jnp.dot(a, b, preferred_element_type=f32)


def loop(start, stop, body):
    def step(i, carry):
        body(i)
        return carry

    lax.fori_loop(start, stop, step, 0)


def thirds(x):
    high = x.astype(bf16)
    rest = x - high.astype(f32)
    middle = rest.astype(bf16)
    low = (rest - middle.astype(f32)).astype(bf16)
    return high, middle, low


def chan_copy(src, dst, send, recv, peer):
    return pltpu.make_async_remote_copy(
        src_ref=src, dst_ref=dst, send_sem=send, recv_sem=recv,
        device_id=(lax.axis_index("win"), peer), device_id_type=MESH,
    )


def win_copy(src, dst, send, recv, peer):
    return pltpu.make_async_remote_copy(
        src_ref=src, dst_ref=dst, send_sem=send, recv_sem=recv,
        device_id=(peer, lax.axis_index("chan")), device_id_type=MESH,
    )


def middle(
    spec, keep, band, near, share, sources, order, quads, own,
    low, high, white, outgoing, mixed, chosen, regroup,
    halo_send, halo_recv, all_send, all_recv, own_send, own_recv, win_send, win_recv,
):
    me = lax.axis_index("chan")
    group = lax.axis_index("win")

    barrier = pltpu.get_barrier_semaphore()

    def greet_chan(k):
        pl.semaphore_signal(barrier, inc=1, device_id=(group, lax.rem(me + k, BLK)), device_id_type=MESH)

    def greet_win(k):
        pl.semaphore_signal(barrier, inc=1, device_id=(lax.rem(group + k, WIN), me), device_id_type=MESH)

    loop(1, BLK, greet_chan)
    loop(1, WIN, greet_win)
    pl.semaphore_wait(barrier, BLK + WIN - 2)

    right, left = lax.rem(me + 1, BLK), lax.rem(me + BLK - 1, BLK)

    def to_right(w):
        return chan_copy(spec.at[w, pl.ds(C - HALO, HALO)], low.at[w], halo_send.at[0, w], halo_recv.at[0, w], right)

    def to_left(w):
        return chan_copy(spec.at[w, pl.ds(0, HALO)], high.at[w], halo_send.at[1, w], halo_recv.at[1, w], left)

    def send_halo(w):
        @pl.when(me < BLK - 1)
        def _():
            to_right(w).start()

        @pl.when(me > 0)
        def _():
            to_left(w).start()


    loop(0, W, send_halo)

    @pl.when(me == 0)
    def _():
        low[...] = jnp.zeros_like(low)

    @pl.when(me == BLK - 1)
    def _():
        high[...] = jnp.zeros_like(high)

    def window(w):
        @pl.when(me > 0)
        def _():
            to_right(w).wait_recv()

        @pl.when(me < BLK - 1)
        def _():
            to_left(w).wait_recv()

        padded = jnp.concatenate([low[w], spec[w], high[w]], axis=0)
        taps = band[...]
        parts = thirds(padded)
        filtered = (mxu(taps, parts[0]) + mxu(taps, parts[1]) + mxu(taps, parts[2])) * keep[...]
        real, imag = filtered[:, :F], filtered[:, F:]
        magnitude = jnp.sqrt(real * real + imag * imag)
        sums = mxu(jnp.concatenate(thirds(magnitude), axis=0), near[...])
        amplitude = (sums[:C] + sums[C : 2 * C] + sums[2 * C :]) * share[...]
        divisor = amplitude + 1e-06
        out = jnp.concatenate([real / divisor, imag / divisor], axis=1)
        white[w] = out
        own[group, pl.ds(pl.multiple_of(w * C, C), C), :] = out.astype(bf16)

    loop(0, W, window)

    tiles = F // 128
    per_tile = 128 // BINS
    lane = iota((C, 128), 1) // BINS

    def regroup_tile(t):
        part, tile = t // tiles, lax.rem(t, tiles)
        columns = pl.ds(pl.multiple_of(t * 128, 128), 128)
        values = [white[w, :, columns] for w in range(W)]
        for m in range(per_tile):
            total = jnp.zeros((C, 128), f32)
            for w in range(W):
                shift = (w - m) * BINS % 128
                moved = pltpu.roll(values[w], shift, 1) if shift else values[w]
                total = jnp.where(lane == w, moved, total)
            outgoing[tile * per_tile + m, :, pl.ds(pl.multiple_of(part * 128, 128), 128)] = total.astype(bf16)

    loop(0, 2 * tiles, regroup_tile)

    def exchange(k):
        peer = lax.rem(me + k, BLK)
        return chan_copy(outgoing.at[peer], mixed.at[me], all_send.at[k], all_recv.at[k], peer)

    def exchange_start(k):
        exchange(k).start()

    loop(1, BLK, exchange_start)

    def share_own(k):
        peer = lax.rem(group + k, WIN)
        return win_copy(own.at[group], own.at[group], own_send.at[k], own_recv.at[k], peer)

    def own_start(k):
        share_own(k).start()

    loop(1, WIN, own_start)
    mixed[me] = outgoing[me]

    def exchange_wait(k):
        exchange(k).wait_recv()

    loop(1, BLK, exchange_wait)
    wanted = jnp.where(iota((WIN * S, BLK * C), 1) == sources[...], 1.0, 0.0).astype(bf16)
    picked = mxu(wanted, mixed[...].reshape(BLK * C, 2 * W * BINS)).astype(bf16)
    chosen[...] = picked.reshape(WIN, S, 2 * W * BINS)

    def trade(k):
        peer = lax.rem(group + k, WIN)
        return win_copy(chosen.at[peer], regroup.at[group], win_send.at[k], win_recv.at[k], peer)

    def trade_start(k):
        trade(k).start()

    loop(1, WIN, trade_start)
    regroup[group] = chosen[group]

    def trade_wait(k):
        trade(k).wait_recv()

    loop(1, WIN, trade_wait)
    arranged = mxu(regroup[0], order[0])
    for g in range(1, WIN):
        arranged += mxu(regroup[g], order[g])
    for q in range(BINS // PACK):
        quads[q] = arranged[:, q * 256 : (q + 1) * 256].astype(bf16)

    def finish_win(k):
        trade(k).wait_send()
        share_own(k).wait()

    def finish_chan(k):
        exchange(k).wait_send()

    def finish_halo(w):
        @pl.when(me < BLK - 1)
        def _():
            to_right(w).wait_send()

        @pl.when(me > 0)
        def _():
            to_left(w).wait_send()


    loop(1, WIN, finish_win)
    loop(1, BLK, finish_chan)
    loop(0, W, finish_halo)


def gather_cross(
    quads, own, far_cos, far_sin, near_cos, near_sin, stacked, inverse,
    held, turned, wide, crossed, send, recv,
):
    me = lax.axis_index("chan")
    group = lax.axis_index("win")
    y, z, x = me // (NZ * NX), lax.rem(me // NX, NZ), lax.rem(me, NX)

    def at(yy, zz, xx):
        return (lax.rem(yy + NY, NY) * NZ + lax.rem(zz, NZ)) * NX + lax.rem(xx + NX, NX)

    y_up, y_down, x_up, x_down, z_over = at(y + 1, z, x), at(y - 1, z, x), at(y, z, x + 1), at(y, z, x - 1), at(y, z + 1, x)

    barrier = pltpu.get_barrier_semaphore()
    for peer in (y_up, y_down, x_up, x_down, z_over):
        pl.semaphore_signal(barrier, inc=1, device_id=(group, peer), device_id_type=MESH)
    pl.semaphore_wait(barrier, 5)

    first = ((y_up, y_down), (x_up, x_down))
    last = ((x_up, x_down), (y_up, y_down))
    per_half = BINS // PACK // 2

    def piece(block, half):
        return held.at[block, pl.ds(half * per_half, per_half)]

    def hop(block, half, slot, peer, src=None):
        src = piece(block, half) if src is None else src
        return chan_copy(src, piece(block, half), send.at[block, half, slot], recv.at[block, half], peer)

    def own_piece(half):
        return quads.at[pl.ds(half * per_half, per_half)]

    def arrived(block, half):
        hop(block, half, 0, z_over).wait_recv()

    def cross(block, half):
        for j in range(per_half):
            quad = block * (2 * per_half) + half * per_half + j
            rows = pl.ds(pl.multiple_of(quad * S, S), S)
            result = mxu(held[block, half * per_half + j], wide[quad])
            crossed[0, rows, :] = result[:, :128]
            crossed[1, rows, :] = result[:, 128:]

    def spread_last(block, half, src=None):
        hop(block, half, 3, last[half][0], src).start()
        hop(block, half, 4, last[half][1], src).start()

    def spread(block, half, src=None):
        hop(block, half, 1, first[half][0], src).start()
        hop(block, half, 2, first[half][1], src).start()
        spread_last(block, half, src)

    def walk(i):
        k = i // NZ
        k = jnp.where(k > 1, 5 - k, k)
        return lax.rem(y + k, NY), lax.rem(x + k, NX), lax.rem(i, NZ)

    for half in (0, 1):
        hop(me, half, 0, z_over, own_piece(half)).start()
    for half in (0, 1):
        spread(me, half, own_piece(half))
    for q in range(2 * per_half):
        held[me, q] = quads[q]

    tiles = F // 128

    def turn_tile(t):
        part_tile, eight = t // 8, lax.rem(t, 8)
        part, tile = part_tile // tiles, lax.rem(part_tile, tiles)
        block = own[pl.ds(pl.multiple_of(eight * 128, 128), 128), pl.ds(pl.multiple_of(part_tile * 128, 128), 128)]
        turned[pl.ds(tile * 128 * 16 + part * 8 + eight, 128, stride=16), :] = block.astype(f32).T

    loop(0, 2 * tiles * 8, turn_tile)

    for half in (0, 1):
        arrived(z_over, half)
        spread(z_over, half)

    lane = iota((8, 128), 1) // 32
    blank = jnp.zeros((16, 128), bf16)

    def widen(quad):
        for b in range(PACK):
            base = pl.multiple_of((quad * PACK + b) * 16, 16)
            real, imag = turned[pl.ds(base, 8), :], turned[pl.ds(base + 8, 8), :]
            reals = [real] + [pltpu.roll(real, 32 * k, 1) for k in range(1, 4)]
            imags = [imag] + [pltpu.roll(imag, 32 * k, 1) for k in range(1, 4)]
            seat = 2 * (b % 2)
            zero = jnp.zeros_like(real)
            for p in range(4):
                to_left, to_right = (seat - p) % 4, (seat + 1 - p) % 4
                upper = jnp.where(lane == seat, reals[to_left], jnp.where(lane == seat + 1, imags[to_right], zero))
                lower = jnp.where(lane == seat, imags[to_left], jnp.where(lane == seat + 1, -reals[to_right], zero))
                tile = jnp.concatenate([upper, lower], axis=0).astype(bf16)
                rows = pl.ds(p * 64 + b * 16, 16)
                wide[quad, rows, pl.ds(128 * (b // 2), 128)] = tile
                wide[quad, rows, pl.ds(128 * (1 - b // 2), 128)] = blank

    loop(0, QUADS // 2, widen)

    def near_block(half, step, zz):
        return at(y + step, zz, x) if half == 0 else at(y, zz, x + step)

    def far_block(half, step, yy, zz):
        return at(yy, zz, x + step) if half == 0 else at(y + step, zz, yy)

    for zz in (z, z + 1):
        for half in (0, 1):
            for step in (-1, 1):
                block = near_block(half, step, zz)
                arrived(block, half)
                which = lax.rem(zz, NZ)
                moves = which == (0 if step == -1 else 1)

                @pl.when(moves)
                def _():
                    hop(block, half, 1 if step == -1 else 2, first[half][0 if step == -1 else 1]).start()

                spread_last(block, half)

    loop(QUADS // 2, QUADS, widen)

    for zz in (0, 1):
        for half in (0, 1):
            block = near_block(half, 2, zz)
            arrived(block, half)
            spread_last(block, half)

    def far_pass(i):
        yy, xx, zz = walk(i)
        for half in (0, 1):
            for step in (-1, 1):
                block = far_block(half, step, yy if half == 0 else xx, zz)
                arrived(block, half)

                @pl.when(zz == (0 if step == -1 else 1))
                def _():
                    hop(block, half, 3 if step == -1 else 4, last[half][0 if step == -1 else 1]).start()

                cross(block, half)

    loop(0, NY * NZ, far_pass)

    for a in range(LAGS // 128):
        inverse[:, a * 128 : (a + 1) * 128] = (
            far_cos[:, a : a + 1] * near_cos[...] - far_sin[:, a : a + 1] * near_sin[...]
        ).astype(bf16)

    def cross_near(i):
        yy, xx, zz = walk(i)
        cross(at(yy, zz, x), 0)
        cross(at(y, zz, xx), 1)

    loop(0, NY * NZ, cross_near)

    def far_last(i):
        yy, xx, zz = walk(i)
        for half in (0, 1):
            block = far_block(half, 2, yy if half == 0 else xx, zz)
            arrived(block, half)
            cross(block, half)

    loop(0, NY * NZ, far_last)

    def turn_source(s):
        rows = pl.ds(pl.multiple_of(s * C, C), C)
        for h in range(2):
            flipped = crossed[h, pl.ds(s, QUADS, stride=S), :].T.astype(bf16)
            for k in range(4):
                stacked[rows, (h * 4 + k) * 128 : (h * 4 + k + 1) * 128] = flipped[k * 32 : (k + 1) * 32]

    loop(0, S, turn_source)

    def sent(block, half, slot):
        hop(block, half, slot, z_over).wait_send()

    for half in (0, 1):
        sent(me, half, 0)
        for zz in (0, 1):
            for slot in (1, 2):
                sent(at(y, zz, x), half, slot)
        sent(near_block(half, -1, 0), half, 1)
        sent(near_block(half, 1, 1), half, 2)

    def sent_far(i):
        yy, xx, zz = walk(i)
        for half in (0, 1):
            block = at(yy, zz, x) if half == 0 else at(y, zz, xx)
            sent(block, half, 3)
            sent(block, half, 4)
            along = yy if half == 0 else xx

            @pl.when(zz == 0)
            def _():
                sent(far_block(half, -1, along, 0), half, 3)

            @pl.when(zz == 1)
            def _():
                sent(far_block(half, 1, along, 1), half, 4)


    loop(0, NY * NZ, sent_far)


def turn(bins, steps):
    phase = jnp.mod(bins * steps, L).astype(f32) * (2.0 * math.pi / L)
    return jnp.cos(phase), jnp.sin(phase)


def forward_table():
    bins = K0 + jnp.arange(F, dtype=i32)
    step = 64
    ca, sa = turn(bins[None, :], step * jnp.arange(L // step, dtype=i32)[:, None])
    cb, sb = turn(bins[None, :], jnp.arange(step, dtype=i32)[:, None])
    ca, sa = jnp.concatenate([ca, ca], 1), jnp.concatenate([sa, sa], 1)
    near_cos, near_sin = jnp.concatenate([cb, -sb], 1), jnp.concatenate([sb, cb], 1)
    ca, sa, near_cos, near_sin = lax.optimization_barrier((ca, sa, near_cos, near_sin))
    table = ca[:, None] * near_cos[None] - sa[:, None] * near_sin[None]
    return table.reshape(L, 2 * F).astype(bf16)


def inverse_parts():
    bins = K0 + PACK * jnp.arange(QUADS, dtype=i32)[None, :] + jnp.arange(PACK, dtype=i32)[:, None]
    bins = bins[:, :, None]
    ca, sa = turn(bins, 128 * jnp.arange(LAGS // 128, dtype=i32) - LAGS // 2)
    cb, sb = turn(bins, jnp.arange(128, dtype=i32))
    both = lambda a, b: jnp.stack([a, b], axis=1).reshape(2 * F, a.shape[-1])
    return both(ca, ca), both(sa, sa), both(cb, -sb), both(sb, cb)


def make_band(filter_taps):
    kernel = jnp.concatenate([-filter_taps[:HALO], jnp.ones((1,), bf16), -filter_taps[HALO:]]).astype(f32)
    offset = iota((C, C + 2 * HALO), 1) - iota((C, C + 2 * HALO), 0)
    choose = offset[:, :, None] == jnp.arange(2 * HALO + 1, dtype=i32)
    return jnp.sum(jnp.where(choose, kernel, 0.0), axis=2).astype(bf16)


def lane_order():
    source = jnp.arange(WIN * 2 * W * BINS, dtype=i32)
    group, rest = source // (2 * W * BINS), source % (2 * W * BINS)
    part, rest = rest // (W * BINS), rest % (W * BINS)
    window, one = rest // BINS, rest % BINS
    target = (one // PACK) * 256 + (window % 4) * 64 + (one % PACK) * 16 + part * 8 + group * 2 + window // 4
    lanes = jnp.arange(WIN * 2 * W * BINS, dtype=i32)
    return (target[:, None] == lanes[None, :]).astype(bf16).reshape(WIN, 2 * W * BINS, WIN * 2 * W * BINS)


def per_device(traces, filter_taps, good_channels, source_index):
    keep = good_channels.astype(f32)
    spectrum = mxu(traces.reshape(W * C, L), forward_table())
    spectrum = spectrum.reshape(W, C, 2 * F) * keep[None, :, None]

    bins = jnp.arange(F, dtype=i32)
    near = (jnp.abs(bins[:, None] - bins[None, :]) <= SMOOTH).astype(f32)
    share = 1.0 / jnp.sum(near, axis=0, keepdims=True)
    vmem = pl.BlockSpec(memory_space=pltpu.VMEM)
    dma = pltpu.SemaphoreType.DMA
    quads, own = pl.pallas_call(
        middle,
        out_shape=(
            jax.ShapeDtypeStruct((BINS // PACK, S, 256), bf16),
            jax.ShapeDtypeStruct((WIN, W * C, 2 * F), bf16),
        ),
        in_specs=[vmem] * 7,
        out_specs=(vmem, vmem),
        scratch_shapes=[
            pltpu.VMEM((W, HALO, 2 * F), f32),
            pltpu.VMEM((W, HALO, 2 * F), f32),
            pltpu.VMEM((W, C, 2 * F), f32),
            pltpu.VMEM((BLK, C, 2 * W * BINS), bf16),
            pltpu.VMEM((BLK, C, 2 * W * BINS), bf16),
            pltpu.VMEM((WIN, S, 2 * W * BINS), bf16),
            pltpu.VMEM((WIN, S, 2 * W * BINS), bf16),
            dma((2, W)), dma((2, W)), dma((BLK,)), dma((BLK,)),
            dma((WIN,)), dma((WIN,)), dma((WIN,)), dma((WIN,)),
        ],
        compiler_params=pltpu.CompilerParams(
            collective_id=0, has_side_effects=True, vmem_limit_bytes=24 << 20
        ),
        name="middle",
    )(
        spectrum, keep[:, None], make_band(filter_taps), near.astype(bf16), share,
        source_index.astype(i32)[:, None], lane_order(),
    )

    halves = 2
    stacked, inverse = pl.pallas_call(
        gather_cross,
        out_shape=(
            jax.ShapeDtypeStruct((S * C, 2 * F), bf16),
            jax.ShapeDtypeStruct((2 * F, LAGS), bf16),
        ),
        in_specs=[vmem] * 6,
        out_specs=(vmem, vmem),
        scratch_shapes=[
            pltpu.VMEM((BLK, BINS // PACK, S, 256), bf16),
            pltpu.VMEM((F * 16, 128), f32),
            pltpu.VMEM((QUADS, 256, 256), bf16),
            pltpu.VMEM((2, QUADS * S, 128), f32),
            dma((BLK, halves, 5)), dma((BLK, halves)),
        ],
        compiler_params=pltpu.CompilerParams(
            collective_id=1, has_side_effects=True, vmem_limit_bytes=56 << 20
        ),
        name="gather_cross",
    )(quads, own.reshape(WIN * W * C, 2 * F), *inverse_parts())

    scaling = 1.0 / math.sqrt(F * W * WIN)
    lagged = mxu(stacked, inverse) * scaling
    return lagged.reshape(S, C, LAGS)


def solution(mesh):
    placed = (P("win", "chan", None), P(), P("chan"), P())
    return jax.shard_map(
        per_device, mesh=mesh, in_specs=placed, out_specs=P("win", "chan", None), check_vma=False
    )
```

time: 659 us -> 154 us (0.23)
  waiting for transfers between devices: 415 us -> 0 us
  Pallas kernels: 0 us -> 118 us
  other arithmetic: 118 us -> 11.2 us
  local copies, waits for them, and re-layouts: 55.6 us -> 4.96 us
  matrix products: 48.7 us -> 19.5 us
  between operations: 13.6 us -> 0.16 us
    reduce_scatter x1 -> x0, waiting for transfers between devices: 260 us -> none  [per_device(): lax.psum_scatter(cross(picked, whitened), 'win', scatter_dimension=0, til...]
    all_gather x1 -> x0, waiting for transfers between devices: 155 us -> none  [per_device(): everything = lax.all_gather(whitened, 'chan', axis=1, tiled=True)]
    pallas_call x0 -> x2, Pallas kernels: none -> 118 us  [the longest x1 63.2 us: per_device(): pl.pallas_call(gather_cross, out_shape=(jax.ShapeDtypeStruct((S * C, 2 *...]
    another operation x2, other arithmetic: 85.7 us -> 1.07 us  [inverse_parts(): both = lambda a, b: jnp.stack([a, b], axis=1).reshape(2 * F, a.shape[-1])]
    concatenate x5 -> x0, local copies, waits for them, and re-layouts: 52.8 us -> none  [the longest x1 32.3 us: cross(): return jnp.concatenate([real_sum, imag_sum], axis=-1)]
    dot_general x6 -> x2, matrix products: 48.7 us -> 19.5 us  [mxu(): return jnp.dot(a, b, preferred_element_type=f32)]
    concatenate x4 -> x2, other arithmetic: 22.8 us -> 0.16 us  [the longest x1 0.11 us: forward_table(): ca, sa = (jnp.concatenate([ca, ca], 1), jnp.concatenate([sa, sa], 1))]
  transfers between devices with their start and end apart: 4 -> 0, of which waited for: 2 -> 0; matrix products, arithmetic and copies ran while one was open for 14% -> 0% of each run, Pallas kernels for 0% -> 0%
where the time goes in v2:
time: 154 us
  Pallas kernels  118 us (77%)
  matrix products  19.5 us (13%)
  other arithmetic  11.2 us (7%)
  local copies, waits for them, and re-layouts  4.96 us (3%)
    pallas_call x1, Pallas kernels, per_device(): pl.pallas_call(gather_cross, out_shape=(jax.ShapeDtypeStruct((S * C, 2 *...  63.2 us
    pallas_call x1, Pallas kernels, per_device(): pl.pallas_call(middle, out_shape=(jax.ShapeDtypeStruct((BINS // PACK, S,...  54.6 us
    dot_general x2, matrix products, mxu(): return jnp.dot(a, b, preferred_element_type=f32)  19.5 us
    convert_element_type x1, other arithmetic, forward_table(): return table.reshape(L, 2 * F).astype(bf16)  4.4 us

profile of v2, /device:TPU:4, one launch (start us, length us, event | category | flops | bytes accessed | tf_op | source)
XLA Modules:
  0.0 153.6 jit_solution(3526133181845050876)
XLA Ops:
  0.0 0.8 slice_negate_fusion.1
  0.8 0.1 maximum_convert_fusion
  0.9 0.7 convert_bitcast_fusion
  1.6 0.1 convert_reduce_fusion
  1.8 0.1 copy.12.keep
  1.9 0.1 select_reduce_fusion.band
  2.0 0.2 fusion.28
  2.2 0.8 copy.13.sources
  3.1 0.5 fusion.19
  3.6 0.1 pad_maximum_fusion.5
  3.7 1.1 copy.14
  4.7 1.1 fusion.12
  5.8 0.1 pad_maximum_fusion.2
  5.9 1.0 copy.15
  6.9 0.1 convert_convert_fusion.near
  7.0 1.1 fusion.5
  8.2 1.1 pad_maximum_fusion.1
  9.3 0.4 fusion.order
  9.7 0.0 copy-start.2
  9.7 4.4 %subtract_convert_fusion = bf16[120,64,1024]{2,1,0:T(8,128)(2,1)S(1)} fusion(f32[64,1024]{1,0:T(8,128)S(1)} %get-tuple-element.16, f32[120,1024]{1,0:T(8,128)S(1)} %get-tuple-element.15, f32[64,1024]{1,0:T(8,128)S(1)} %get-tuple-element.14, f32[120,1024]{1,0:T(8,128)S(1)} %get-tuple-element.13), kind=kLoop, calls=%fused_computation | loop fusion | flops 31457280 | bytes 17235968 | tf_op jit(solution)/shard_map/convert_element_type | solution.py:449
  14.1 0.0 copy-done.2
  14.1 4.2 %fusion.54 = f32[1024,256]{0,1:T(8,128)S(1)} fusion(bf16[256,7680]{1,0:T(8,128)(2,1)S(1)} %bitcast.28, bf16[7680,1024]{1,0:T(8,128)(2,1)S(1)} %bitcast.21), kind=kOutput, calls=%fused_computation.118 | convolution fusion | flops 4026531840 | bytes 20709376 | tf_op jit(solution)/shard_map/dot_general | solution.py:39
  18.3 0.2 broadcast_multiply_fusion.spec
  18.5 54.6 %middle.1 = (bf16[4,64,256]{2,1,0:T(8,128)(2,1)S(1)}, bf16[4,256,1024]{2,1,0:T(8,128)(2,1)S(1)}) custom-call(f32[8,32,1024]{2,1,0:T(8,128)S(1)} %broadcast_multiply_fusion.spec, f32[32,1]{1,0:T(8,128)S(1)} %copy.12.keep, bf16[32,64]{1,0:T(8,128)(2,1)S(1)} %select_reduce_fusion.band, bf16[512,512]{1,0:T(8,128)(2,1)S(1)} %convert_convert_fusion.near, ...), custom_call_target="tpu_custom_call" | custom-call | tf_op jit(solution)/shard_map/middle/pallas_call | solution.py:488
  73.1 0.0 copy-start
  73.1 1.3 copy-done
  74.4 0.0 copy-start.1
  74.4 0.7 copy-done.1
  75.0 63.2 %gather_cross.1 = (bf16[2048,1024]{1,0:T(8,128)(2,1)}, bf16[1024,2048]{1,0:T(8,128)(2,1)}) custom-call(bf16[4,64,256]{2,1,0:T(8,128)(2,1)} %copy-done.1, bf16[1024,1024]{1,0:T(8,128)(2,1)} %bitcast.19, f32[1024,16]{1,0:T(8,128)} %bitcast.24, f32[1024,16]{1,0:T(8,128)} %bitcast.25, f32[1024,128]{1,0:T(8,128)} %bitcast.23, f32[1024,128]{1,0:T(8,128)} %bitcast.22), custom_call_target="tpu_custom_call" | custom-call | tf_op jit(solution)/shard_map/gather_cross/pallas_call | solution.py:517
  138.3 15.3 %convolution_multiply_fusion = f32[2048,2048]{1,0:T(8,128)} fusion(bf16[2048,1024]{1,0:T(8,128)(2,1)} %get-tuple-element.19, bf16[1024,2048]{1,0:T(8,128)(2,1)} %get-tuple-element.20), kind=kOutput, calls=%fused_computation.1 | convolution fusion | flops 8594128896 | bytes 25165824 | tf_op jit(solution)/shard_map/dot_general | solution.py:39
  (9 shorter events, 0.1 us)
Async XLA Ops:
  9.7 4.4 %copy-start.2 = (bf16[8,32,7680]{2,1,0:T(8,128)(2,1)S(1)}, bf16[8,32,7680]{2,1,0:T(8,128)(2,1)}, u32[]{:S(2)}) copy-start(bf16[8,32,7680]{2,1,0:T(8,128)(2,1)} %param.4) | copy-start | bytes 11796484
  73.1 1.3 copy-start
  74.4 0.7 copy-start.1

commit v3 on v2

v3 whole, which is shorter than its diff:
```python
import functools
import math

import jax
import jax.numpy as jnp
from jax import lax
from jax.experimental import pallas as pl
from jax.experimental.pallas import tpu as pltpu
from jax.sharding import PartitionSpec as P

L = 7680
F = 512
LAGS = 2048
HALO = 16
SMOOTH = 64
K0 = 31

WIN = 4
BLK = 32
NX = 4
NZ = 2
NY = 4
W = 8
C = 32
S = 64
BINS = F // BLK
QUADS = F // 4
PACK = 4
PAIR = 2
DEEP = 2 * W * WIN
MESH = pl.DeviceIdType.MESH
f32, bf16, i32 = jnp.float32, jnp.bfloat16, jnp.int32


def iota(shape, dim):
    return lax.broadcasted_iota(i32, shape, dim)


def mxu(a, b):
    return jnp.dot(a, b, preferred_element_type=f32)


def loop(start, stop, body):
    def step(i, carry):
        body(i)
        return carry

    lax.fori_loop(start, stop, step, 0)


def thirds(x):
    high = x.astype(bf16)
    rest = x - high.astype(f32)
    middle = rest.astype(bf16)
    low = (rest - middle.astype(f32)).astype(bf16)
    return high, middle, low


def chan_copy(src, dst, send, recv, peer):
    return pltpu.make_async_remote_copy(
        src_ref=src, dst_ref=dst, send_sem=send, recv_sem=recv,
        device_id=(lax.axis_index("win"), peer), device_id_type=MESH,
    )


def win_copy(src, dst, send, recv, peer):
    return pltpu.make_async_remote_copy(
        src_ref=src, dst_ref=dst, send_sem=send, recv_sem=recv,
        device_id=(peer, lax.axis_index("chan")), device_id_type=MESH,
    )


def diagonal(row, count):
    return jnp.sum(jnp.where(iota((count, count), 0) == iota((count, count), 1), row, 0.0), axis=1, keepdims=True)


def whole(
    spec, good, taps, near, share, sources, order, far_cos, far_sin, near_cos, near_sin, crossed_hbm, inverse_hbm,
    low, high, white, outgoing, mixed, chosen, regroup, own, quads, held, turned, wide, crossed, inverse,
    halo_send, halo_recv, all_send, all_recv, own_send, own_recv, win_send, win_recv, send, recv, out_sem,
):
    me = lax.axis_index("chan")
    group = lax.axis_index("win")
    y, z, x = me // (NZ * NX), lax.rem(me // NX, NZ), lax.rem(me, NX)
    layer, core = group // 2, lax.rem(group, 2)
    sibling, across, diagonal_group = layer * 2 + 1 - core, (1 - layer) * 2 + core, (1 - layer) * 2 + 1 - core

    barrier = pltpu.get_barrier_semaphore()

    def greet_chan(k):
        pl.semaphore_signal(barrier, inc=1, device_id=(group, lax.rem(me + k, BLK)), device_id_type=MESH)

    def greet_win(k):
        pl.semaphore_signal(barrier, inc=1, device_id=(lax.rem(group + k, WIN), me), device_id_type=MESH)

    loop(1, BLK, greet_chan)
    loop(1, WIN, greet_win)
    pl.semaphore_wait(barrier, BLK + WIN - 2)

    right, left = lax.rem(me + 1, BLK), lax.rem(me + BLK - 1, BLK)

    def to_right(w):
        return chan_copy(spec.at[w, pl.ds(C - HALO, HALO)], low.at[w], halo_send.at[0, w], halo_recv.at[0, w], right)

    def to_left(w):
        return chan_copy(spec.at[w, pl.ds(0, HALO)], high.at[w], halo_send.at[1, w], halo_recv.at[1, w], left)

    def send_halo(w):
        @pl.when(me < BLK - 1)
        def _():
            to_right(w).start()

        @pl.when(me > 0)
        def _():
            to_left(w).start()

    loop(0, W, send_halo)

    @pl.when(me == 0)
    def _():
        low[...] = jnp.zeros_like(low)

    @pl.when(me == BLK - 1)
    def _():
        high[...] = jnp.zeros_like(high)

    for b in range(PACK):
        bins = slice(b * QUADS, (b + 1) * QUADS)
        fc, fs = far_cos[:, bins].T, far_sin[:, bins].T
        nc, ns = near_cos[bins, :], near_sin[bins, :]
        for a in range(LAGS // 128):
            columns = slice(a * 128, (a + 1) * 128)
            ca, sa = fc[:, a : a + 1], fs[:, a : a + 1]
            inverse[2 * b * QUADS : (2 * b + 1) * QUADS, columns] = (ca * nc - sa * ns).astype(bf16)
            inverse[(2 * b + 1) * QUADS : (2 * b + 2) * QUADS, columns] = -(sa * nc + ca * ns).astype(bf16)
    inverse_out = pltpu.make_async_copy(inverse, inverse_hbm, out_sem.at[0])
    inverse_out.start()

    offset = iota((C, C + 2 * HALO), 1) - iota((C, C + 2 * HALO), 0)
    band = jnp.where(offset == HALO, 1.0, 0.0)
    for o in range(HALO):
        band = jnp.where(offset == o, -taps[o], band)
        band = jnp.where(offset == HALO + 1 + o, -taps[HALO + o], band)
    band = band.astype(bf16)
    keep = diagonal(good[...].astype(f32), C)

    def to_group(hop, w, whose, peer):
        rows = pl.ds(pl.multiple_of(w * C, C), C)
        return win_copy(own.at[whose, rows], own.at[whose, rows], own_send.at[hop, w], own_recv.at[hop, w], peer)

    def window(w):
        @pl.when(me > 0)
        def _():
            to_right(w).wait_recv()

        @pl.when(me < BLK - 1)
        def _():
            to_left(w).wait_recv()

        padded = jnp.concatenate([low[w], spec[w], high[w]], axis=0)
        parts = thirds(padded)
        filtered = (mxu(band, parts[0]) + mxu(band, parts[1]) + mxu(band, parts[2])) * keep
        real, imag = filtered[:, :F], filtered[:, F:]
        magnitude = jnp.sqrt(real * real + imag * imag)
        sums = mxu(jnp.concatenate(thirds(magnitude), axis=0), near[...])
        amplitude = (sums[:C] + sums[C : 2 * C] + sums[2 * C :]) * share[...]
        divisor = amplitude + 1e-06
        out = jnp.concatenate([real / divisor, imag / divisor], axis=1)
        white[w] = out
        own[group, pl.ds(pl.multiple_of(w * C, C), C), :] = out.astype(bf16)
        to_group(0, w, group, across).start()
        to_group(1, w, group, sibling).start()

    loop(0, W, window)

    tiles = F // 128
    per_tile = 128 // BINS
    lane = iota((C, 128), 1) // BINS

    def regroup_tile(t):
        part, tile = t // tiles, lax.rem(t, tiles)
        columns = pl.ds(pl.multiple_of(t * 128, 128), 128)
        values = [white[w, :, columns] for w in range(W)]
        for m in range(per_tile):
            total = jnp.zeros((C, 128), f32)
            for w in range(W):
                shift = (w - m) * BINS % 128
                moved = pltpu.roll(values[w], shift, 1) if shift else values[w]
                total = jnp.where(lane == w, moved, total)
            outgoing[tile * per_tile + m, :, pl.ds(pl.multiple_of(part * 128, 128), 128)] = total.astype(bf16)

    loop(0, 2 * tiles, regroup_tile)

    def exchange(k):
        peer = lax.rem(me + k, BLK)
        return chan_copy(outgoing.at[peer], mixed.at[me], all_send.at[k], all_recv.at[k], peer)

    loop(1, BLK, lambda k: exchange(k).start())
    mixed[me] = outgoing[me]

    def turn_group(whose):
        def turn_tile(part_tile):
            part, tile = part_tile // tiles, lax.rem(part_tile, tiles)
            columns = pl.ds(pl.multiple_of(part_tile * 128, 128), 128)
            for half in range(2):
                block = own[whose, half * 128 : (half + 1) * 128, columns]
                start = tile * 128 * 16 + part * 8 + whose * 2 + half
                turned[pl.ds(start, 128, stride=16), :] = block.astype(f32).T

        loop(0, 2 * tiles, turn_tile)

    turn_group(group)
    wanted = jnp.where(iota((WIN * S, BLK * C), 1) == diagonal(sources[...].astype(f32), WIN * S).astype(i32), 1.0, 0.0).astype(bf16)
    loop(0, W, lambda w: to_group(1, w, sibling, sibling).wait_recv())
    turn_group(sibling)

    loop(1, BLK, lambda k: exchange(k).wait_recv())
    picked = mxu(wanted, mixed[...].reshape(BLK * C, 2 * W * BINS)).astype(bf16)
    chosen[...] = picked.reshape(WIN, S, 2 * W * BINS)

    def trade(k):
        peer = lax.rem(group + k, WIN)
        return win_copy(chosen.at[peer], regroup.at[group], win_send.at[k], win_recv.at[k], peer)

    loop(1, WIN, lambda k: trade(k).start())
    regroup[group] = chosen[group]

    def relay(w):
        to_group(0, w, across, across).wait_recv()
        to_group(2, w, across, sibling).start()

    loop(0, W, relay)
    turn_group(across)
    loop(1, WIN, lambda k: trade(k).wait_recv())
    arranged = mxu(regroup[0], order[0])
    for g in range(1, WIN):
        arranged += mxu(regroup[g], order[g])
    for q in range(BINS // PACK):
        quads[q] = arranged[:, q * 256 : (q + 1) * 256].astype(bf16)

    def at(yy, zz, xx):
        return (lax.rem(yy + NY, NY) * NZ + lax.rem(zz, NZ)) * NX + lax.rem(xx + NX, NX)

    y_up, y_down, x_up, x_down, z_over = at(y + 1, z, x), at(y - 1, z, x), at(y, z, x + 1), at(y, z, x - 1), at(y, z + 1, x)

    first = ((y_up, y_down), (x_up, x_down))
    last = ((x_up, x_down), (y_up, y_down))
    per_half = BINS // PACK // 2

    def piece(block, half):
        return held.at[block, pl.ds(half * per_half, per_half)]

    def hop(block, half, slot, peer, src=None):
        src = piece(block, half) if src is None else src
        return chan_copy(src, piece(block, half), send.at[block, half, slot], recv.at[block, half], peer)

    def own_piece(half):
        return quads.at[pl.ds(half * per_half, per_half)]

    def arrived(block, half):
        hop(block, half, 0, z_over).wait_recv()

    def spread_last(block, half, src=None):
        hop(block, half, 3, last[half][0], src).start()
        hop(block, half, 4, last[half][1], src).start()

    def spread(block, half, src=None):
        hop(block, half, 1, first[half][0], src).start()
        hop(block, half, 2, first[half][1], src).start()
        spread_last(block, half, src)

    def walk(i):
        k = i // NZ
        k = jnp.where(k > 1, 5 - k, k)
        return lax.rem(y + k, NY), lax.rem(x + k, NX), lax.rem(i, NZ)

    for half in (0, 1):
        hop(me, half, 0, z_over, own_piece(half)).start()
    for half in (0, 1):
        spread(me, half, own_piece(half))
    for q in range(2 * per_half):
        held[me, q] = quads[q]

    loop(0, W, lambda w: to_group(2, w, diagonal_group, sibling).wait_recv())
    turn_group(diagonal_group)

    for half in (0, 1):
        arrived(z_over, half)
        spread(z_over, half)

    lane32 = iota((16, 128), 1) // 32
    seats = [jnp.where(lane32 == k, 1.0, 0.0).astype(bf16) for k in range(4)]

    def widen(quad):
        for b in range(PACK):
            base = pl.multiple_of((quad * PACK + b) * 16, 16)
            real, imag = turned[pl.ds(base, 8), :], turned[pl.ds(base + 8, 8), :]
            straight, crosswise = [], []
            for k in range(4):
                r = pltpu.roll(real, 32 * k, 1) if k else real
                i = pltpu.roll(imag, 32 * k, 1) if k else imag
                straight.append(jnp.concatenate([r, i], axis=0).astype(bf16))
                crosswise.append(jnp.concatenate([i, -r], axis=0).astype(bf16))
            seat = 2 * (b % PAIR)
            for p in range(4):
                tile = straight[(seat - p) % 4] * seats[seat] + crosswise[(seat + 1 - p) % 4] * seats[seat + 1]
                wide[quad * 2 + b // PAIR, pl.ds(p * 32 + (b % PAIR) * 16, 16), :] = tile

    loop(0, QUADS, widen)

    def result_out(first_row, count):
        rows = pl.ds(pl.multiple_of(first_row, S), count)
        return pltpu.make_async_copy(crossed.at[:, rows], crossed_hbm.at[:, rows], out_sem.at[1])

    def cross(block, half):
        for j in range(per_half):
            quad = block * (2 * per_half) + half * per_half + j
            rows = pl.ds(pl.multiple_of(quad * S, S), S)
            for h in range(2):
                crossed[h, rows, :] = mxu(held[block, half * per_half + j, :, h * 128 : (h + 1) * 128], wide[quad * 2 + h])
        result_out((block * 2 + half) * per_half * S, per_half * S).start()

    def near_block(half, step, zz):
        return at(y + step, zz, x) if half == 0 else at(y, zz, x + step)

    def far_block(half, step, along, zz):
        return at(along, zz, x + step) if half == 0 else at(y + step, zz, along)

    for zz in (z, z + 1):
        for half in (0, 1):
            for step in (-1, 1):
                block = near_block(half, step, zz)
                arrived(block, half)

                @pl.when(lax.rem(zz, NZ) == (0 if step == -1 else 1))
                def _():
                    hop(block, half, 1 if step == -1 else 2, first[half][0 if step == -1 else 1]).start()

                spread_last(block, half)

    for zz in (0, 1):
        for half in (0, 1):
            block = near_block(half, 2, zz)
            arrived(block, half)
            spread_last(block, half)

    def far_pass(i):
        yy, xx, zz = walk(i)
        for half in (0, 1):
            for step in (-1, 1):
                block = far_block(half, step, yy if half == 0 else xx, zz)
                arrived(block, half)

                @pl.when(zz == (0 if step == -1 else 1))
                def _():
                    hop(block, half, 3 if step == -1 else 4, last[half][0 if step == -1 else 1]).start()

                cross(block, half)

    loop(0, NY * NZ, far_pass)

    def cross_near(i):
        yy, xx, zz = walk(i)
        cross(at(yy, zz, x), 0)
        cross(at(y, zz, xx), 1)

    loop(0, NY * NZ, cross_near)

    def far_last(i):
        yy, xx, zz = walk(i)
        for half in (0, 1):
            block = far_block(half, 2, yy if half == 0 else xx, zz)
            arrived(block, half)
            cross(block, half)

    loop(0, NY * NZ, far_last)

    def finish_win(k):
        trade(k).wait_send()

    def finish_own(w):
        to_group(0, w, group, across).wait_send()
        to_group(1, w, group, sibling).wait_send()
        to_group(2, w, across, sibling).wait_send()

    def finish_halo(w):
        @pl.when(me < BLK - 1)
        def _():
            to_right(w).wait_send()

        @pl.when(me > 0)
        def _():
            to_left(w).wait_send()

    loop(1, WIN, finish_win)
    loop(0, W, finish_own)
    loop(1, BLK, lambda k: exchange(k).wait_send())
    loop(0, W, finish_halo)

    def sent(block, half, slot):
        hop(block, half, slot, z_over).wait_send()

    for half in (0, 1):
        sent(me, half, 0)
        for zz in (0, 1):
            for slot in (1, 2):
                sent(at(y, zz, x), half, slot)
        sent(near_block(half, -1, 0), half, 1)
        sent(near_block(half, 1, 1), half, 2)

    def sent_far(i):
        yy, xx, zz = walk(i)
        for half in (0, 1):
            block = at(yy, zz, x) if half == 0 else at(y, zz, xx)
            sent(block, half, 3)
            sent(block, half, 4)
            along = yy if half == 0 else xx

            @pl.when(zz == 0)
            def _():
                sent(far_block(half, -1, along, 0), half, 3)

            @pl.when(zz == 1)
            def _():
                sent(far_block(half, 1, along, 1), half, 4)

    loop(0, NY * NZ, sent_far)
    inverse_out.wait()
    result_out(0, QUADS * S).wait()


def to_lags(scaling, crossed, inverse, out, stacked):
    for s in range(8):
        for h in range(2):
            flipped = crossed[h, :, s, :].T.astype(bf16)
            for k in range(4):
                stacked[s * C : (s + 1) * C, (h * 4 + k) * 128 : (h * 4 + k + 1) * 128] = flipped[k * 32 : (k + 1) * 32]
    out[...] = (mxu(stacked[...], inverse[...]) * scaling).reshape(8, C, LAGS)


def turn(bins, steps):
    phase = jnp.mod(bins * steps, L).astype(f32) * (2.0 * math.pi / L)
    return jnp.cos(phase), jnp.sin(phase)


def forward_table():
    bins = K0 + jnp.arange(F, dtype=i32)
    step = 64
    ca, sa = turn(bins[None, :], step * jnp.arange(L // step, dtype=i32)[:, None])
    cb, sb = turn(bins[None, :], jnp.arange(step, dtype=i32)[:, None])
    ca, sa = jnp.concatenate([ca, ca], 1), jnp.concatenate([sa, sa], 1)
    near_cos, near_sin = jnp.concatenate([cb, -sb], 1), jnp.concatenate([sb, cb], 1)
    ca, sa, near_cos, near_sin = lax.optimization_barrier((ca, sa, near_cos, near_sin))
    table = ca[:, None] * near_cos[None] - sa[:, None] * near_sin[None]
    return table.reshape(L, 2 * F).astype(bf16)


def inverse_parts():
    bins = (K0 + PACK * jnp.arange(QUADS, dtype=i32)[None, :] + jnp.arange(PACK, dtype=i32)[:, None]).reshape(F)
    far = turn(bins[None, :], 128 * jnp.arange(LAGS // 128, dtype=i32)[:, None] - LAGS // 2)
    return far + turn(bins[:, None], jnp.arange(128, dtype=i32)[None, :])


def lane_order():
    source = jnp.arange(WIN * 2 * W * BINS, dtype=i32)
    group, rest = source // (2 * W * BINS), source % (2 * W * BINS)
    part, rest = rest // (W * BINS), rest % (W * BINS)
    window, one = rest // BINS, rest % BINS
    target = (one // PAIR) * 128 + (window % 4) * 32 + (one % PAIR) * 16 + part * 8 + group * 2 + window // 4
    lanes = jnp.arange(WIN * 2 * W * BINS, dtype=i32)
    return (target[:, None] == lanes[None, :]).astype(bf16).reshape(WIN, 2 * W * BINS, WIN * 2 * W * BINS)


def per_device(traces, filter_taps, good_channels, source_index):
    keep = good_channels.astype(f32)
    spectrum = mxu(traces.reshape(W * C, L), forward_table())
    spectrum = spectrum.reshape(W, C, 2 * F) * keep[None, :, None]

    bins = jnp.arange(F, dtype=i32)
    near = (jnp.abs(bins[:, None] - bins[None, :]) <= SMOOTH).astype(f32)
    share = 1.0 / jnp.sum(near, axis=0, keepdims=True)
    vmem = pl.BlockSpec(memory_space=pltpu.VMEM)
    smem = pl.BlockSpec(memory_space=pltpu.SMEM)
    anywhere = pl.BlockSpec(memory_space=pl.ANY)
    dma = pltpu.SemaphoreType.DMA
    crossed, inverse = pl.pallas_call(
        whole,
        out_shape=(
            jax.ShapeDtypeStruct((2, QUADS * S, 128), f32),
            jax.ShapeDtypeStruct((2 * F, LAGS), bf16),
        ),
        in_specs=[vmem, vmem, smem] + [vmem] * 8,
        out_specs=(anywhere, anywhere),
        scratch_shapes=[
            pltpu.VMEM((W, HALO, 2 * F), f32),
            pltpu.VMEM((W, HALO, 2 * F), f32),
            pltpu.VMEM((W, C, 2 * F), f32),
            pltpu.VMEM((BLK, C, 2 * W * BINS), bf16),
            pltpu.VMEM((BLK, C, 2 * W * BINS), bf16),
            pltpu.VMEM((WIN, S, 2 * W * BINS), bf16),
            pltpu.VMEM((WIN, S, 2 * W * BINS), bf16),
            pltpu.VMEM((WIN, W * C, 2 * F), bf16),
            pltpu.VMEM((BINS // PACK, S, 256), bf16),
            pltpu.VMEM((BLK, BINS // PACK, S, 256), bf16),
            pltpu.VMEM((F * 16, 128), f32),
            pltpu.VMEM((QUADS * 2, 128, 128), bf16),
            pltpu.VMEM((2, QUADS * S, 128), f32),
            pltpu.VMEM((2 * F, LAGS), bf16),
            dma((2, W)), dma((2, W)), dma((BLK,)), dma((BLK,)),
            dma((3, W)), dma((3, W)), dma((WIN,)), dma((WIN,)),
            dma((BLK, 2, 5)), dma((BLK, 2)), dma((2,)),
        ],
        compiler_params=pltpu.CompilerParams(
            collective_id=0, has_side_effects=True, vmem_limit_bytes=52 << 20
        ),
        name="whole",
    )(
        spectrum, good_channels.astype(i32)[None, :], filter_taps.astype(f32), near.astype(bf16), share,
        source_index.astype(i32)[None, :], lane_order(), *inverse_parts(),
    )

    return pl.pallas_call(
        functools.partial(to_lags, 1.0 / math.sqrt(F * W * WIN)),
        grid=(S // 8,),
        out_shape=jax.ShapeDtypeStruct((S, C, LAGS), f32),
        in_specs=[
            pl.BlockSpec((2, QUADS, 8, 128), lambda i: (0, 0, i, 0)),
            pl.BlockSpec((2 * F, LAGS), lambda i: (0, 0), pipeline_mode=pl.Buffered(1)),
        ],
        out_specs=pl.BlockSpec((8, C, LAGS), lambda i: (i, 0, 0)),
        scratch_shapes=[pltpu.VMEM((8 * C, 2 * F), bf16)],
        compiler_params=pltpu.CompilerParams(vmem_limit_bytes=32 << 20),
        name="to_lags",
    )(crossed.reshape(2, QUADS, S, 128), inverse)


def solution(mesh):
    placed = (P("win", "chan", None), P(), P("chan"), P())
    return jax.shard_map(
        per_device, mesh=mesh, in_specs=placed, out_specs=P("win", "chan", None), check_vma=False
    )
```

time: 154 us -> 129 us (0.84)
  matrix products: 19.5 us -> 4.55 us
  Pallas kernels: 118 us -> 106 us
    dot_general x2 -> x1, matrix products: 19.5 us -> 4.55 us  [mxu(): return jnp.dot(a, b, preferred_element_type=f32)]
    pallas_call x2, Pallas kernels: 118 us -> 106 us  [the longest x1 89.7 us: per_device(): pl.pallas_call(whole, out_shape=(jax.ShapeDtypeStruct((2, QUADS * S, 128)...]
    unnamed x6 -> x10, local copies, waits for them, and re-layouts: 1.97 us -> 5.58 us
    another operation x2 -> x0, local copies, waits for them, and re-layouts: 2.09 us -> none  [inverse_parts(): both = lambda a, b: jnp.stack([a, b], axis=1).reshape(2 * F, a.shape[-1])]
    convert_element_type x1 -> x2, other arithmetic: 0.08 us -> 1.63 us  [the longest x1 0.82 us: per_device(): keep = good_channels.astype(f32)]
where the time goes in v3:
time: 129 us
  Pallas kernels  106 us (82%)
  other arithmetic  12.4 us (10%)
  local copies, waits for them, and re-layouts  5.58 us (4%)
  matrix products  4.55 us (4%)
    pallas_call x1, Pallas kernels, per_device(): pl.pallas_call(whole, out_shape=(jax.ShapeDtypeStruct((2, QUADS * S, 128)...  89.7 us
    pallas_call x1, Pallas kernels, per_device(): pl.pallas_call(functools.partial(to_lags, 1.0 / math.sqrt(F * W * WIN)),...  16.6 us
    unnamed x10, local copies, waits for them, and re-layouts  5.58 us
    dot_general x1, matrix products, mxu(): return jnp.dot(a, b, preferred_element_type=f32)  4.55 us
    convert_element_type x1, other arithmetic, forward_table(): return table.reshape(L, 2 * F).astype(bf16)  4.38 us
    sin x4, other arithmetic, turn(): return (jnp.cos(phase), jnp.sin(phase))  2.96 us

profile of v3, /device:TPU:4, one launch (start us, length us, event | category | flops | bytes accessed | tf_op | source)
XLA Modules:
  0.0 128.8 jit_solution(518967085388751758)
XLA Ops:
  0.0 0.0 copy-start.4
  0.0 0.8 convert_element_type.63.taps
  0.8 0.8 convert_element_type.62
  1.7 0.1 convert_reduce_fusion
  1.9 0.2 fusion.27
  2.1 0.5 fusion.19
  2.7 1.1 fusion.12
  3.8 0.1 pad_maximum_fusion
  3.9 1.1 fusion.5
  5.0 0.1 convert_convert_fusion.near
  5.1 1.7 %fusion.order = bf16[4,256,1024]{2,1,0:T(8,128)(2,1)} fusion(s32[4,256]{1,0:T(4,128)S(1)} %fusion.35), kind=kLoop, calls=%fused_computation.2 | loop fusion | flops 2097152 | bytes 2101248 | tf_op jit(solution)/shard_map/convert_element_type | solution.py:471
  6.8 4.4 %subtract_convert_fusion = bf16[120,64,1024]{2,1,0:T(8,128)(2,1)S(1)} fusion(f32[64,1024]{1,0:T(8,128)S(1)} %get-tuple-element.14, f32[120,1024]{1,0:T(8,128)S(1)} %get-tuple-element.13, f32[64,1024]{1,0:T(8,128)S(1)} %get-tuple-element.12, f32[120,1024]{1,0:T(8,128)S(1)} %get-tuple-element.11), kind=kLoop, calls=%fused_computation | loop fusion | flops 31457280 | bytes 17235968 | tf_op jit(solution)/shard_map/convert_element_type | solution.py:455
  11.2 0.0 copy-done.4
  11.2 0.0 copy-start.2
  11.2 0.0 copy-start.3
  11.3 4.5 %fusion.53 = f32[1024,256]{0,1:T(8,128)S(1)} fusion(bf16[256,7680]{1,0:T(8,128)(2,1)S(1)} %bitcast.19, bf16[7680,1024]{1,0:T(8,128)(2,1)S(1)} %bitcast.17), kind=kOutput, calls=%fused_computation.105 | convolution fusion | flops 4026531840 | bytes 20709376 | tf_op jit(solution)/shard_map/dot_general | solution.py:40
  15.8 1.2 broadcast_multiply_fusion.spec
  17.0 0.0 copy-done.2
  17.0 0.0 copy-done.3
  17.0 89.7 %whole.1 = (f32[2,8192,128]{2,1,0:T(8,128)}, bf16[1024,2048]{1,0:T(8,128)(2,1)}) custom-call(f32[8,32,1024]{2,1,0:T(8,128)} %broadcast_multiply_fusion.spec, s32[1,32]{1,0:T(1,128)S(1)} %bitcast.16, f32[32]{0:T(128)S(1)} %convert_element_type.63.taps, bf16[512,512]{1,0:T(8,128)(2,1)S(1)} %convert_convert_fusion.near, f32[1,512]{1,0:T(1,128)S(1)} %bitcast.14, ...), custom_call_target="tpu_custom_call" | custom-call | tf_op jit(solution)/shard_map/whole/pallas_call | solution.py:486
  106.7 0.0 copy-start
  106.7 3.4 %copy-done = f32[2,8192,128]{2,1,0:T(8,128)S(1)} copy-done((f32[2,8192,128]{2,1,0:T(8,128)S(1)}, f32[2,8192,128]{2,1,0:T(8,128)}, u32[]{:S(2)}) %copy-start) | copy-done | bytes 8388632
  110.1 0.0 copy-start.1
  110.1 2.2 %copy-done.1 = bf16[1024,2048]{1,0:T(8,128)(2,1)S(1)} copy-done((bf16[1024,2048]{1,0:T(8,128)(2,1)S(1)}, bf16[1024,2048]{1,0:T(8,128)(2,1)}, u32[]{:S(2)}) %copy-start.1) | copy-done | bytes 4194328
  112.3 16.6 %to_lags.1 = f32[64,32,2048]{2,1,0:T(8,128)} custom-call(f32[2,128,64,128]{3,2,1,0:T(8,128)S(1)} %bitcast.13, bf16[1024,2048]{1,0:T(8,128)(2,1)S(1)} %copy-done.1), custom_call_target="tpu_custom_call" | custom-call | tf_op jit(solution)/shard_map/to_lags/pallas_call | solution.py:522
  (8 shorter events, 0.1 us)
Async XLA Ops:
  0.0 11.2 %copy-start.4 = (bf16[8,32,7680]{2,1,0:T(8,128)(2,1)S(1)}, bf16[8,32,7680]{2,1,0:T(8,128)(2,1)}, u32[]{:S(2)}) copy-start(bf16[8,32,7680]{2,1,0:T(8,128)(2,1)} %param.4) | copy-start | bytes 11796484
  11.2 5.8 %copy-start.2 = (s32[256]{0:T(256)S(1)}, s32[256]{0:T(256)}, u32[]{:S(2)}) copy-start(s32[256]{0:T(256)} %param.7) | copy-start | bytes 3076
  11.2 5.8 %copy-start.3 = (s32[32]{0:T(128)S(1)}, s32[32]{0:T(128)}, u32[]{:S(2)}) copy-start(s32[32]{0:T(128)} %param.6) | copy-start | bytes 388
  106.7 3.4 %copy-start = (f32[2,8192,128]{2,1,0:T(8,128)S(1)}, f32[2,8192,128]{2,1,0:T(8,128)}, u32[]{:S(2)}) copy-start(f32[2,8192,128]{2,1,0:T(8,128)} %get-tuple-element.15) | copy-start | bytes 25165828
  110.1 2.2 %copy-start.1 = (bf16[1024,2048]{1,0:T(8,128)(2,1)S(1)}, bf16[1024,2048]{1,0:T(8,128)(2,1)}, u32[]{:S(2)}) copy-start(bf16[1024,2048]{1,0:T(8,128)(2,1)} %get-tuple-element.16.inverse) | copy-start | bytes 12582916

commit v4 on v3

v4 whole, which is shorter than its diff:
```python
import functools
import math

import jax
import jax.numpy as jnp
from jax import lax
from jax.experimental import pallas as pl
from jax.experimental.pallas import tpu as pltpu
from jax.sharding import PartitionSpec as P

L = 7680
F = 512
LAGS = 2048
HALO = 16
SMOOTH = 64
K0 = 31

WIN = 4
BLK = 32
NX = 4
NZ = 2
NY = 4
W = 8
C = 32
S = 64
BINS = F // BLK
QUADS = F // 4
PACK = 4
PAIR = 2
STEP = 64
DEEP = 2 * W * WIN
MESH = pl.DeviceIdType.MESH
f32, bf16, i32 = jnp.float32, jnp.bfloat16, jnp.int32


def iota(shape, dim):
    return lax.broadcasted_iota(i32, shape, dim)


def mxu(a, b):
    return jnp.dot(a, b, preferred_element_type=f32)


def loop(start, stop, body):
    def step(i, carry):
        body(i)
        return carry

    lax.fori_loop(start, stop, step, 0)


def thirds(x):
    high = x.astype(bf16)
    rest = x - high.astype(f32)
    middle = rest.astype(bf16)
    low = (rest - middle.astype(f32)).astype(bf16)
    return high, middle, low


def chan_copy(src, dst, send, recv, peer):
    return pltpu.make_async_remote_copy(
        src_ref=src, dst_ref=dst, send_sem=send, recv_sem=recv,
        device_id=(lax.axis_index("win"), peer), device_id_type=MESH,
    )


def win_copy(src, dst, send, recv, peer):
    return pltpu.make_async_remote_copy(
        src_ref=src, dst_ref=dst, send_sem=send, recv_sem=recv,
        device_id=(peer, lax.axis_index("chan")), device_id_type=MESH,
    )


def diagonal(row, count):
    return jnp.sum(jnp.where(iota((count, count), 0) == iota((count, count), 1), row, 0.0), axis=1, keepdims=True)


def whole(
    traces, good, taps, sources, row_cos, row_sin, step_cos, step_sin, far_cos, far_sin, near_cos, near_sin,
    crossed_hbm, inverse_hbm,
    rows, table, spec, low, high, filtered, magnitudes, outgoing, mixed, chosen, regroup, own, quads, held, turned, wide,
    crossed, inverse,
    halo_send, halo_recv, all_send, all_recv, own_send, own_recv, win_send, win_recv, send, recv, out_sem,
):
    me = lax.axis_index("chan")
    group = lax.axis_index("win")
    y, z, x = me // (NZ * NX), lax.rem(me // NX, NZ), lax.rem(me, NX)
    layer, core = group // 2, lax.rem(group, 2)
    sibling, across, diagonal_group = layer * 2 + 1 - core, (1 - layer) * 2 + core, (1 - layer) * 2 + 1 - core

    rows_in = pltpu.make_async_copy(traces, rows, out_sem.at[2])
    rows_in.start()
    barrier = pltpu.get_barrier_semaphore()

    def greet_chan(k):
        pl.semaphore_signal(barrier, inc=1, device_id=(group, lax.rem(me + k, BLK)), device_id_type=MESH)

    def greet_win(k):
        pl.semaphore_signal(barrier, inc=1, device_id=(lax.rem(group + k, WIN), me), device_id_type=MESH)

    loop(1, BLK, greet_chan)
    loop(1, WIN, greet_win)

    offset = iota((C, C + 2 * HALO), 1) - iota((C, C + 2 * HALO), 0)
    weights = taps[...].astype(f32)
    band = jnp.where(offset == HALO, 1.0, 0.0)
    for o in range(HALO):
        band = jnp.where(offset == o, -weights[:, o : o + 1], band)
        band = jnp.where(offset == HALO + 1 + o, -weights[:, HALO + o : HALO + o + 1], band)
    band = jnp.concatenate([band, band, band], axis=1).astype(bf16)
    keep = diagonal(good[...].astype(f32), C)
    beside = jnp.where(jnp.abs(iota((384, 128), 0) - 128 - iota((384, 128), 1)) <= SMOOTH, 1.0, 0.0).astype(bf16)
    magnitudes[:, 0:128] = jnp.zeros((3 * W * C, 128), bf16)
    magnitudes[:, 640:768] = jnp.zeros((3 * W * C, 128), bf16)

    @pl.when(me == 0)
    def _():
        low[...] = jnp.zeros_like(low)

    @pl.when(me == BLK - 1)
    def _():
        high[...] = jnp.zeros_like(high)

    tiles = F // 128
    per_tile = 128 // BINS
    right, left = lax.rem(me + 1, BLK), lax.rem(me + BLK - 1, BLK)

    def to_right(n):
        return chan_copy(spec.at[n, :, pl.ds(C - HALO, HALO)], low.at[n], halo_send.at[0, n], halo_recv.at[0, n], right)

    def to_left(n):
        return chan_copy(spec.at[n, :, pl.ds(0, HALO)], high.at[n], halo_send.at[1, n], halo_recv.at[1, n], left)

    def tile_of(n):
        return pl.ds(pl.multiple_of(n * 128, 128), 128)

    def transform(n):
        columns = tile_of(n)
        cb, sb = step_cos[:, columns], step_sin[:, columns]

        def table_rows(i):
            eight = pl.ds(pl.multiple_of(i * 8, 8), 8)
            cas, sas = row_cos[eight, columns], row_sin[eight, columns]
            for u in range(8):
                ca, sa = cas[u : u + 1], sas[u : u + 1]
                at_rows = pl.ds(pl.multiple_of((i * 8 + u) * STEP, STEP), STEP)
                table[at_rows, 0:128] = (ca * cb - sa * sb).astype(bf16)
                table[at_rows, 128:256] = (-sa * cb - ca * sb).astype(bf16)

        loop(0, L // STEP // 8, table_rows)

        @pl.when(n == 0)
        def _():
            rows_in.wait()

        spec[n] = mxu(rows[...], table[...]).reshape(W, C, 256) * keep

        @pl.when(n == 0)
        def _():
            pl.semaphore_wait(barrier, BLK + WIN - 2)

        @pl.when(me < BLK - 1)
        def _():
            to_right(n).start()

        @pl.when(me > 0)
        def _():
            to_left(n).start()

    def filter_tile(n):
        @pl.when(me > 0)
        def _():
            to_right(n).wait_recv()

        @pl.when(me < BLK - 1)
        def _():
            to_left(n).wait_recv()

        for w in range(W):
            padded = jnp.concatenate([low[n, w], spec[n, w], high[n, w]], axis=0)
            out = mxu(band, jnp.concatenate(thirds(padded), axis=0)) * keep
            filtered[n, w * C : (w + 1) * C, :] = out
            real, imag = out[:, :128], out[:, 128:]
            for k, part in enumerate(thirds(jnp.sqrt(real * real + imag * imag))):
                magnitudes[(k * W + w) * C : (k * W + w + 1) * C, tile_of(n + 1)] = part

    lane = iota((C, 128), 1) // BINS

    def exchange(k):
        peer = lax.rem(me + k, BLK)
        return chan_copy(outgoing.at[peer], mixed.at[me], all_send.at[k], all_recv.at[k], peer)

    def to_group(hop, tile, whose, peer):
        return win_copy(own.at[whose, tile], own.at[whose, tile], own_send.at[hop, tile], own_recv.at[hop, tile], peer)

    def turn_tile(whose, part, tile):
        for half in range(2):
            block = own[whose, part * tiles + tile, half * 128 : (half + 1) * 128, :]
            start = tile * 128 * 16 + part * 8 + whose * 2 + half
            turned[pl.ds(start, 128, stride=16), :] = block.astype(f32).T

    def turn_group(whose):
        def both(tile):
            turn_tile(whose, 0, tile)
            turn_tile(whose, 1, tile)

        loop(0, tiles, both)

    def home(n, m):
        return (m // NZ) * NZ * NX + (m % NZ) * NX + lax.rem(n + m // NZ, NX)

    def place(block):
        yy, zz, xx = block // (NZ * NX), lax.rem(block // NX, NZ), lax.rem(block, NX)
        return lax.rem(xx - yy + NX, NX) * per_tile + yy * NZ + zz

    def whiten_tile(n):
        sums = mxu(magnitudes[:, pl.ds(pl.multiple_of(n * 128, 128), 384)], beside)
        bins = iota((1, 128), 1) + n * 128
        count = 1 + jnp.minimum(bins, SMOOTH) + jnp.minimum(F - 1 - bins, SMOOTH)
        total = sums[: W * C] + sums[W * C : 2 * W * C] + sums[2 * W * C :]
        inverse_amplitude = 1.0 / (total * (1.0 / count.astype(f32)) + 1e-06)
        for part in range(2):
            values = filtered[n, :, part * 128 : (part + 1) * 128] * inverse_amplitude
            own[group, part * tiles + n] = values.astype(bf16)
            windows = [values[w * C : (w + 1) * C] for w in range(W)]
            for m in range(per_tile):
                packed = jnp.zeros((C, 128), f32)
                for w in range(W):
                    shift = (w - m) * BINS % 128
                    moved = pltpu.roll(windows[w], shift, 1) if shift else windows[w]
                    packed = jnp.where(lane == w, moved, packed)
                outgoing[home(n, m), :, part * 128 : (part + 1) * 128] = packed.astype(bf16)
        for m in range(per_tile):
            peer = home(n, m)

            @pl.when(peer != me)
            def _():
                exchange(lax.rem(peer - me + BLK, BLK)).start()

        for part in range(2):
            to_group(0, part * tiles + n, group, across).start()
            to_group(1, part * tiles + n, group, sibling).start()

    def stage(n):
        @pl.when(n < tiles)
        def _():
            transform(n)

        @pl.when((n >= 2) & (n < tiles + 2))
        def _():
            filter_tile(n - 2)

        @pl.when(n >= 3)
        def _():
            whiten_tile(n - 3)

    loop(0, tiles + 3, stage)
    mixed[me] = outgoing[me]

    wanted = jnp.where(iota((WIN * S, BLK * C), 1) == diagonal(sources[...].astype(f32), WIN * S).astype(i32), 1.0, 0.0).astype(bf16)
    span = 2 * W * BINS
    source = iota((span, 1), 0)
    window, one = lax.rem(source // BINS, W), lax.rem(source, BINS)
    target = (one // PAIR) * 128 + lax.rem(window, 4) * 32 + lax.rem(one, PAIR) * 16 + source // (W * BINS) * 8 + window // 4
    order = jnp.where(iota((span, WIN * span), 1) == target, 1.0, 0.0).astype(bf16)
    turn_group(group)
    loop(0, 2 * tiles, lambda t: to_group(1, t, sibling, sibling).wait_recv())
    turn_group(sibling)

    loop(1, BLK, lambda k: exchange(k).wait_recv())
    picked = mxu(wanted, mixed[...].reshape(BLK * C, 2 * W * BINS)).astype(bf16)
    chosen[...] = picked.reshape(WIN, S, 2 * W * BINS)

    def trade(k):
        peer = lax.rem(group + k, WIN)
        return win_copy(chosen.at[peer], regroup.at[group], win_send.at[k], win_recv.at[k], peer)

    loop(1, WIN, lambda k: trade(k).start())
    regroup[group] = chosen[group]

    def relay(t):
        to_group(0, t, across, across).wait_recv()
        to_group(2, t, across, sibling).start()

    loop(0, 2 * tiles, relay)
    turn_group(across)
    loop(1, WIN, lambda k: trade(k).wait_recv())
    arranged = mxu(regroup[0], order)
    for g in range(1, WIN):
        arranged += pltpu.roll(mxu(regroup[g], order), 2 * g, 1)
    for q in range(BINS // PACK):
        quads[q] = arranged[:, q * 256 : (q + 1) * 256].astype(bf16)

    def at(yy, zz, xx):
        return (lax.rem(yy + NY, NY) * NZ + lax.rem(zz, NZ)) * NX + lax.rem(xx + NX, NX)

    y_up, y_down, x_up, x_down, z_over = at(y + 1, z, x), at(y - 1, z, x), at(y, z, x + 1), at(y, z, x - 1), at(y, z + 1, x)

    first = ((y_up, y_down), (x_up, x_down))
    last = ((x_up, x_down), (y_up, y_down))
    per_half = BINS // PACK // 2

    def piece(block, half):
        return held.at[block, pl.ds(half * per_half, per_half)]

    def hop(block, half, slot, peer, src=None):
        src = piece(block, half) if src is None else src
        return chan_copy(src, piece(block, half), send.at[block, half, slot], recv.at[block, half], peer)

    def own_piece(half):
        return quads.at[pl.ds(half * per_half, per_half)]

    def arrived(block, half):
        hop(block, half, 0, z_over).wait_recv()

    def spread_last(block, half, src=None):
        hop(block, half, 3, last[half][0], src).start()
        hop(block, half, 4, last[half][1], src).start()

    def spread(block, half, src=None):
        hop(block, half, 1, first[half][0], src).start()
        hop(block, half, 2, first[half][1], src).start()
        spread_last(block, half, src)

    def walk(i):
        k = i // NZ
        k = jnp.where(k > 1, 5 - k, k)
        return lax.rem(y + k, NY), lax.rem(x + k, NX), lax.rem(i, NZ)

    for half in (0, 1):
        hop(me, half, 0, z_over, own_piece(half)).start()
    for half in (0, 1):
        spread(me, half, own_piece(half))
    for q in range(2 * per_half):
        held[me, q] = quads[q]

    loop(0, 2 * tiles, lambda t: to_group(2, t, diagonal_group, sibling).wait_recv())
    turn_group(diagonal_group)

    for half in (0, 1):
        arrived(z_over, half)
        spread(z_over, half)

    lane32 = iota((16, 128), 1) // 32
    seats = [jnp.where(lane32 == k, 1.0, 0.0).astype(bf16) for k in range(4)]

    def widen(quad):
        for b in range(PACK):
            base = pl.multiple_of((quad * PACK + b) * 16, 16)
            real, imag = turned[pl.ds(base, 8), :], turned[pl.ds(base + 8, 8), :]
            straight, crosswise = [], []
            for k in range(4):
                r = pltpu.roll(real, 32 * k, 1) if k else real
                i = pltpu.roll(imag, 32 * k, 1) if k else imag
                straight.append(jnp.concatenate([r, i], axis=0).astype(bf16))
                crosswise.append(jnp.concatenate([i, -r], axis=0).astype(bf16))
            seat = 2 * (b % PAIR)
            for p in range(4):
                tile = straight[(seat - p) % 4] * seats[seat] + crosswise[(seat + 1 - p) % 4] * seats[seat + 1]
                wide[quad * 2 + b // PAIR, pl.ds(p * 32 + (b % PAIR) * 16, 16), :] = tile

    loop(0, QUADS, widen)

    def result_out(first_row, count):
        rows = pl.ds(pl.multiple_of(first_row, S), count)
        return pltpu.make_async_copy(crossed.at[:, rows], crossed_hbm.at[:, rows], out_sem.at[1])

    def cross(block, half):
        for j in range(per_half):
            quad = place(block) * (2 * per_half) + half * per_half + j
            rows = pl.ds(pl.multiple_of(quad * S, S), S)
            for h in range(2):
                crossed[h, rows, :] = mxu(held[block, half * per_half + j, :, h * 128 : (h + 1) * 128], wide[quad * 2 + h])
        result_out((place(block) * 2 + half) * per_half * S, per_half * S).start()

    def near_block(half, step, zz):
        return at(y + step, zz, x) if half == 0 else at(y, zz, x + step)

    def far_block(half, step, along, zz):
        return at(along, zz, x + step) if half == 0 else at(y + step, zz, along)

    for zz in (z, z + 1):
        for half in (0, 1):
            for step in (-1, 1):
                block = near_block(half, step, zz)
                arrived(block, half)

                @pl.when(lax.rem(zz, NZ) == (0 if step == -1 else 1))
                def _():
                    hop(block, half, 1 if step == -1 else 2, first[half][0 if step == -1 else 1]).start()

                spread_last(block, half)

    for zz in (0, 1):
        for half in (0, 1):
            block = near_block(half, 2, zz)
            arrived(block, half)
            spread_last(block, half)

    for b in range(PACK):
        bins = slice(b * QUADS, (b + 1) * QUADS)
        fc, fs = far_cos[:, bins].T, far_sin[:, bins].T
        nc, ns = near_cos[bins, :], near_sin[bins, :]
        for a in range(LAGS // 128):
            columns = slice(a * 128, (a + 1) * 128)
            ca, sa = fc[:, a : a + 1], fs[:, a : a + 1]
            inverse[2 * b * QUADS : (2 * b + 1) * QUADS, columns] = (ca * nc - sa * ns).astype(bf16)
            inverse[(2 * b + 1) * QUADS : (2 * b + 2) * QUADS, columns] = -(sa * nc + ca * ns).astype(bf16)
    inverse_out = pltpu.make_async_copy(inverse, inverse_hbm, out_sem.at[0])
    inverse_out.start()

    def far_pass(i):
        yy, xx, zz = walk(i)
        for half in (0, 1):
            for step in (-1, 1):
                block = far_block(half, step, yy if half == 0 else xx, zz)
                arrived(block, half)

                @pl.when(zz == (0 if step == -1 else 1))
                def _():
                    hop(block, half, 3 if step == -1 else 4, last[half][0 if step == -1 else 1]).start()

                cross(block, half)

    loop(0, NY * NZ, far_pass)

    def cross_near(i):
        yy, xx, zz = walk(i)
        cross(at(yy, zz, x), 0)
        cross(at(y, zz, xx), 1)

    loop(0, NY * NZ, cross_near)

    def far_last(i):
        yy, xx, zz = walk(i)
        for half in (0, 1):
            block = far_block(half, 2, yy if half == 0 else xx, zz)
            arrived(block, half)
            cross(block, half)

    loop(0, NY * NZ, far_last)

    def finish_win(k):
        trade(k).wait_send()

    def finish_own(w):
        to_group(0, w, group, across).wait_send()
        to_group(1, w, group, sibling).wait_send()
        to_group(2, w, across, sibling).wait_send()

    def finish_halo(w):
        @pl.when(me < BLK - 1)
        def _():
            to_right(w).wait_send()

        @pl.when(me > 0)
        def _():
            to_left(w).wait_send()

    loop(1, WIN, finish_win)
    loop(0, 2 * tiles, finish_own)
    loop(1, BLK, lambda k: exchange(k).wait_send())
    loop(0, tiles, finish_halo)

    def sent(block, half, slot):
        hop(block, half, slot, z_over).wait_send()

    for half in (0, 1):
        sent(me, half, 0)
        for zz in (0, 1):
            for slot in (1, 2):
                sent(at(y, zz, x), half, slot)
        sent(near_block(half, -1, 0), half, 1)
        sent(near_block(half, 1, 1), half, 2)

    def sent_far(i):
        yy, xx, zz = walk(i)
        for half in (0, 1):
            block = at(yy, zz, x) if half == 0 else at(y, zz, xx)
            sent(block, half, 3)
            sent(block, half, 4)
            along = yy if half == 0 else xx

            @pl.when(zz == 0)
            def _():
                sent(far_block(half, -1, along, 0), half, 3)

            @pl.when(zz == 1)
            def _():
                sent(far_block(half, 1, along, 1), half, 4)

    loop(0, NY * NZ, sent_far)
    inverse_out.wait()
    result_out(0, QUADS * S).wait()


def to_lags(scaling, crossed, inverse, out, even, odd):
    def both(fill, full):
        out[...] = (mxu(full[...], inverse[...]) * scaling).reshape(8, C, LAGS)
        for s in range(8):
            for h in range(2):
                flipped = crossed[h, :, s, :].T.astype(bf16)
                for k in range(4):
                    columns = slice((h * 4 + k) * 128, (h * 4 + k + 1) * 128)
                    fill[s * C : (s + 1) * C, columns] = flipped[k * 32 : (k + 1) * 32]

    @pl.when(lax.rem(pl.program_id(0), 2) == 0)
    def _():
        both(even, odd)

    @pl.when(lax.rem(pl.program_id(0), 2) == 1)
    def _():
        both(odd, even)


def turn(bins, steps):
    phase = jnp.mod(bins * steps, L).astype(f32) * (2.0 * math.pi / L)
    return jnp.cos(phase), jnp.sin(phase)


def forward_parts():
    bins = (K0 + jnp.arange(F, dtype=i32))[None, :]
    return turn(bins, STEP * jnp.arange(L // STEP, dtype=i32)[:, None]) + turn(bins, jnp.arange(STEP, dtype=i32)[:, None])


def inverse_parts():
    bins = (K0 + PACK * jnp.arange(QUADS, dtype=i32)[None, :] + jnp.arange(PACK, dtype=i32)[:, None]).reshape(F)
    far = turn(bins[None, :], 128 * jnp.arange(LAGS // 128, dtype=i32)[:, None] - LAGS // 2)
    return far + turn(bins[:, None], jnp.arange(128, dtype=i32)[None, :])


def per_device(traces, filter_taps, good_channels, source_index):
    vmem = pl.BlockSpec(memory_space=pltpu.VMEM)
    smem = pl.BlockSpec(memory_space=pltpu.SMEM)
    anywhere = pl.BlockSpec(memory_space=pl.ANY)
    dma = pltpu.SemaphoreType.DMA
    crossed, inverse = pl.pallas_call(
        whole,
        out_shape=(
            jax.ShapeDtypeStruct((2, QUADS * S, 128), f32),
            jax.ShapeDtypeStruct((2 * F, LAGS), bf16),
        ),
        in_specs=[anywhere] + [vmem] * 11,
        out_specs=(anywhere, anywhere),
        scratch_shapes=[
            pltpu.VMEM((W * C, L), bf16),
            pltpu.VMEM((L, 256), bf16),
            pltpu.VMEM((F // 128, W, C, 256), f32),
            pltpu.VMEM((F // 128, W, HALO, 256), f32),
            pltpu.VMEM((F // 128, W, HALO, 256), f32),
            pltpu.VMEM((F // 128, W * C, 256), f32),
            pltpu.VMEM((3 * W * C, F + 256), bf16),
            pltpu.VMEM((BLK, C, 2 * W * BINS), bf16),
            pltpu.VMEM((BLK, C, 2 * W * BINS), bf16),
            pltpu.VMEM((WIN, S, 2 * W * BINS), bf16),
            pltpu.VMEM((WIN, S, 2 * W * BINS), bf16),
            pltpu.VMEM((WIN, 2 * F // 128, W * C, 128), bf16),
            pltpu.VMEM((BINS // PACK, S, 256), bf16),
            pltpu.VMEM((BLK, BINS // PACK, S, 256), bf16),
            pltpu.VMEM((F * 16, 128), f32),
            pltpu.VMEM((QUADS * 2, 128, 128), bf16),
            pltpu.VMEM((2, QUADS * S, 128), f32),
            pltpu.VMEM((2 * F, LAGS), bf16),
            dma((2, F // 128)), dma((2, F // 128)), dma((BLK,)), dma((BLK,)),
            dma((3, 2 * F // 128)), dma((3, 2 * F // 128)), dma((WIN,)), dma((WIN,)),
            dma((BLK, 2, 5)), dma((BLK, 2)), dma((3,)),
        ],
        compiler_params=pltpu.CompilerParams(
            collective_id=0, has_side_effects=True, vmem_limit_bytes=60 << 20
        ),
        name="whole",
    )(
        traces.reshape(W * C, L), good_channels.astype(i32)[None, :], filter_taps[None, :],
        source_index.astype(i32)[None, :], *forward_parts(), *inverse_parts(),
    )

    return pl.pallas_call(
        functools.partial(to_lags, 1.0 / math.sqrt(F * W * WIN)),
        grid=(S // 8 + 1,),
        out_shape=jax.ShapeDtypeStruct((S, C, LAGS), f32),
        in_specs=[
            pl.BlockSpec((2, QUADS, 8, 128), lambda i: (0, 0, jnp.minimum(i, S // 8 - 1), 0)),
            pl.BlockSpec((2 * F, LAGS), lambda i: (0, 0), pipeline_mode=pl.Buffered(1)),
        ],
        out_specs=pl.BlockSpec((8, C, LAGS), lambda i: (jnp.maximum(i - 1, 0), 0, 0)),
        scratch_shapes=[pltpu.VMEM((8 * C, 2 * F), bf16)] * 2,
        compiler_params=pltpu.CompilerParams(vmem_limit_bytes=62 << 20),
        name="to_lags",
    )(crossed.reshape(2, QUADS, S, 128), inverse)


def solution(mesh):
    placed = (P("win", "chan", None), P(), P("chan"), P())
    return jax.shard_map(
        per_device, mesh=mesh, in_specs=placed, out_specs=P("win", "chan", None), check_vma=False
    )
```

time: 129 us -> 115 us (0.89)
  other arithmetic: 12.4 us -> 5.95 us
  local copies, waits for them, and re-layouts: 5.58 us -> 0 us
  matrix products: 4.55 us -> 0 us
  Pallas kernels: 106 us -> 109 us
    convert_element_type x5 -> x0, other arithmetic: 7.83 us -> none  [the longest x1 4.38 us: forward_table(): return table.reshape(L, 2 * F).astype(bf16)]
    unnamed x10 -> x0, local copies, waits for them, and re-layouts: 5.58 us -> none
    dot_general x1 -> x0, matrix products: 4.55 us -> none  [mxu(): return jnp.dot(a, b, preferred_element_type=f32)]
    pallas_call x1, Pallas kernels: 16.6 us -> 19.8 us  [per_device(): pl.pallas_call(functools.partial(to_lags, 1.0 / math.sqrt(F * W * WIN)),...]
    sin x4, other arithmetic: 2.96 us -> 5.93 us  [turn(): return (jnp.cos(phase), jnp.sin(phase))]
where the time goes in v4:
time: 115 us
  Pallas kernels  109 us (95%)
  other arithmetic  5.95 us (5%)
    pallas_call x1, Pallas kernels, per_device(): pl.pallas_call(whole, out_shape=(jax.ShapeDtypeStruct((2, QUADS * S, 128)...  89.1 us
    pallas_call x1, Pallas kernels, per_device(): pl.pallas_call(functools.partial(to_lags, 1.0 / math.sqrt(F * W * WIN)),...  19.8 us
    sin x4, other arithmetic, turn(): return (jnp.cos(phase), jnp.sin(phase))  5.93 us

profile of v4, /device:TPU:4, one launch (start us, length us, event | category | flops | bytes accessed | tf_op | source)
XLA Modules:
  0.0 114.9 jit_solution(12780640156737201416)
XLA Ops:
  0.0 0.8 fusion.25
  0.9 1.3 %fusion.18 = (f32[64,512]{1,0:T(8,128)}, f32[64,512]{1,0:T(8,128)}) fusion(s32[512]{0:T(512)S(1)} %iota_add_fusion), kind=kLoop, calls=%fused_computation.24 | loop fusion | flops 294912 | bytes 264192 | tf_op jit(solution)/shard_map/sin | solution.py:518
  2.1 1.9 %fusion.11 = (f32[120,512]{1,0:T(8,128)}, f32[120,512]{1,0:T(8,128)}) fusion(s32[120]{0:T(128)S(1)} %iota_multiply_fusion, s32[512]{0:T(512)S(1)} %iota_add_fusion), kind=kLoop, calls=%fused_computation.15 | loop fusion | flops 552960 | bytes 494048 | tf_op jit(solution)/shard_map/sin | solution.py:518
  4.0 1.9 %fusion.4 = (f32[512,128]{1,0:T(8,128)}, f32[512,128]{1,0:T(8,128)}) fusion(s32[512]{0:T(512)S(1)} %add_bitcast_fusion), kind=kLoop, calls=%fused_computation.7 | loop fusion | flops 589824 | bytes 526336 | tf_op jit(solution)/shard_map/sin | solution.py:518
  6.0 89.1 %whole.1 = (f32[2,8192,128]{2,1,0:T(8,128)}, bf16[1024,2048]{1,0:T(8,128)(2,1)}) custom-call(bf16[256,7680]{1,0:T(8,128)(2,1)} %bitcast.8, s32[1,32]{1,0:T(1,128)} %bitcast.10, bf16[1,32]{1,0:T(2,128)(2,1)} %bitcast.11, s32[1,256]{1,0:T(1,128)} %bitcast.9, f32[120,512]{1,0:T(8,128)} %get-tuple-element.12.row_cos, f32[120,512]{1,0:T(8,128)} %get-tuple-element.11.row_sin, ...), custom_call_target="tpu_custom_call" | custom-call | tf_op jit(solution)/shard_map/whole/pallas_call | solution.py:537
  95.1 19.8 %to_lags.1 = f32[64,32,2048]{2,1,0:T(8,128)} custom-call(f32[2,128,64,128]{3,2,1,0:T(8,128)} %bitcast.7, bf16[1024,2048]{1,0:T(8,128)(2,1)} %get-tuple-element.8.inverse), custom_call_target="tpu_custom_call" | custom-call | tf_op jit(solution)/shard_map/to_lags/pallas_call | solution.py:577
  (5 shorter events, 0.0 us)

commit v5 on v4

--- a/solution.py
+++ b/solution.py
@@ -1,4 +1,3 @@
-import functools
 import math
 
 import jax
@@ -27,6 +26,7 @@
 QUADS = F // 4
 PACK = 4
 PAIR = 2
+LIMIT = 54
 STEP = 64
 DEEP = 2 * W * WIN
 MESH = pl.DeviceIdType.MESH
@@ -76,9 +76,8 @@
 
 
 def whole(
-    traces, good, taps, sources, row_cos, row_sin, step_cos, step_sin, far_cos, far_sin, near_cos, near_sin,
-    crossed_hbm, inverse_hbm,
-    rows, table, spec, low, high, filtered, magnitudes, outgoing, mixed, chosen, regroup, own, quads, held, turned, wide,
+    traces, good, taps, sources, cosines, sines, stacked_out, inverse_out,
+    row_cos, row_sin, step_cos, step_sin, near_cos, near_sin, far, spread_pair, stacked, rows, table, spec, low, high, filtered, magnitudes, outgoing, mixed, chosen, regroup, own, quads, held, turned, wide,
     crossed, inverse,
     halo_send, halo_recv, all_send, all_recv, own_send, own_recv, win_send, win_recv, send, recv, out_sem,
 ):
@@ -121,6 +120,15 @@
     def _():
         high[...] = jnp.zeros_like(high)
 
+    def sums(a, b):
+        ca, sa, cb, sb = cosines[a, :], sines[a, :], cosines[b, :], sines[b, :]
+        return ca * cb - sa * sb, sa * cb + ca * sb
+
+    for i in range(L // STEP // 8):
+        row_cos[i * 8 : (i + 1) * 8, :], row_sin[i * 8 : (i + 1) * 8, :] = sums(slice(i, i + 1), slice(16, 24))
+    for i in range(STEP // 8):
+        step_cos[i * 8 : (i + 1) * 8, :], step_sin[i * 8 : (i + 1) * 8, :] = sums(slice(24 + i, 25 + i), slice(32, 40))
+
     tiles = F // 128
     per_tile = 128 // BINS
     right, left = lax.rem(me + 1, BLK), lax.rem(me + BLK - 1, BLK)
@@ -196,8 +204,8 @@
     def turn_tile(whose, part, tile):
         for half in range(2):
             block = own[whose, part * tiles + tile, half * 128 : (half + 1) * 128, :]
-            start = tile * 128 * 16 + part * 8 + whose * 2 + half
-            turned[pl.ds(start, 128, stride=16), :] = block.astype(f32).T
+            start = part * F * 8 + tile * 128 * 8 + whose * 2 + half
+            turned[pl.ds(start, 128, stride=8), :] = block.astype(f32).T
 
     def turn_group(whose):
         def both(tile):
@@ -223,13 +231,16 @@
             values = filtered[n, :, part * 128 : (part + 1) * 128] * inverse_amplitude
             own[group, part * tiles + n] = values.astype(bf16)
             windows = [values[w * C : (w + 1) * C] for w in range(W)]
+            for d in (1, 2, 4):
+                clear = lane // d % 2 == 0
+                before = list(windows)
+                for w in range(W):
+                    if not w & d:
+                        a, b = before[w], before[w | d]
+                        windows[w] = jnp.where(clear, a, pltpu.roll(b, d * BINS, 1))
+                        windows[w | d] = jnp.where(clear, pltpu.roll(a, 128 - d * BINS, 1), b)
             for m in range(per_tile):
-                packed = jnp.zeros((C, 128), f32)
-                for w in range(W):
-                    shift = (w - m) * BINS % 128
-                    moved = pltpu.roll(windows[w], shift, 1) if shift else windows[w]
-                    packed = jnp.where(lane == w, moved, packed)
-                outgoing[home(n, m), :, part * 128 : (part + 1) * 128] = packed.astype(bf16)
+                outgoing[home(n, m), :, part * 128 : (part + 1) * 128] = windows[m].astype(bf16)
         for m in range(per_tile):
             peer = home(n, m)
 
@@ -261,8 +272,16 @@
     span = 2 * W * BINS
     source = iota((span, 1), 0)
     window, one = lax.rem(source // BINS, W), lax.rem(source, BINS)
-    target = (one // PAIR) * 128 + lax.rem(window, 4) * 32 + lax.rem(one, PAIR) * 16 + source // (W * BINS) * 8 + window // 4
+    pair, seat = one // PACK * 2 + lax.rem(one, 2), lax.rem(one // 2, 2)
+    target = pair * 128 + lax.rem(window, 4) * 32 + seat * 16 + source // (W * BINS) * 8 + window // 4
     order = jnp.where(iota((span, WIN * span), 1) == target, 1.0, 0.0).astype(bf16)
+    column = iota((1, 1024), 1)
+    kind, part = lax.rem(column // 128, 2), lax.rem(column // 32, 2)
+    origin = jnp.where(kind == part, 0, 128) + column // 256 * 32 + lax.rem(column, 32)
+    sign = jnp.where(kind * part == 1, -1.0, 1.0)
+    for b in range(PAIR):
+        used = jnp.where(lax.rem(column // 64, 2) == b, origin, -1)
+        spread_pair[b] = jnp.where(iota((256, 1024), 0) == used, sign, 0.0).astype(bf16)
     turn_group(group)
     loop(0, 2 * tiles, lambda t: to_group(1, t, sibling, sibling).wait_recv())
     turn_group(sibling)
@@ -341,29 +360,19 @@
         arrived(z_over, half)
         spread(z_over, half)
 
-    lane32 = iota((16, 128), 1) // 32
-    seats = [jnp.where(lane32 == k, 1.0, 0.0).astype(bf16) for k in range(4)]
-
-    def widen(quad):
-        for b in range(PACK):
-            base = pl.multiple_of((quad * PACK + b) * 16, 16)
-            real, imag = turned[pl.ds(base, 8), :], turned[pl.ds(base + 8, 8), :]
-            straight, crosswise = [], []
-            for k in range(4):
-                r = pltpu.roll(real, 32 * k, 1) if k else real
-                i = pltpu.roll(imag, 32 * k, 1) if k else imag
-                straight.append(jnp.concatenate([r, i], axis=0).astype(bf16))
-                crosswise.append(jnp.concatenate([i, -r], axis=0).astype(bf16))
-            seat = 2 * (b % PAIR)
+    def widen(i):
+        start = pl.multiple_of(i * 512, 512)
+        real, imag = turned[pl.ds(start, 512), :], turned[pl.ds(F * 8 + start, 512), :]
+        both = jnp.concatenate([real, imag], axis=1).reshape(16, 2, 16, 256)
+        for b in range(PAIR):
+            spread_rows = mxu(both[:, b].reshape(256, 256).astype(bf16), spread_pair[b])
             for p in range(4):
-                tile = straight[(seat - p) % 4] * seats[seat] + crosswise[(seat + 1 - p) % 4] * seats[seat + 1]
-                wide[quad * 2 + b // PAIR, pl.ds(p * 32 + (b % PAIR) * 16, 16), :] = tile
-
-    loop(0, QUADS, widen)
-
-    def result_out(first_row, count):
-        rows = pl.ds(pl.multiple_of(first_row, S), count)
-        return pltpu.make_async_copy(crossed.at[:, rows], crossed_hbm.at[:, rows], out_sem.at[1])
+                upper = spread_rows[:, p * 256 : p * 256 + 128].reshape(32, 8, 128)
+                lower = spread_rows[:, p * 256 + 128 : p * 256 + 256].reshape(32, 8, 128)
+                tile = jnp.concatenate([upper, lower], axis=1).astype(bf16)
+                wide[pl.ds(pl.multiple_of(i * 32, 32), 32), p * 32 + b * 16 : p * 32 + b * 16 + 16, :] = tile
+
+    loop(0, F * 8 // 512, widen)
 
     def cross(block, half):
         for j in range(per_half):
@@ -371,7 +380,6 @@
             rows = pl.ds(pl.multiple_of(quad * S, S), S)
             for h in range(2):
                 crossed[h, rows, :] = mxu(held[block, half * per_half + j, :, h * 128 : (h + 1) * 128], wide[quad * 2 + h])
-        result_out((place(block) * 2 + half) * per_half * S, per_half * S).start()
 
     def near_block(half, step, zz):
         return at(y + step, zz, x) if half == 0 else at(y, zz, x + step)
@@ -397,17 +405,25 @@
             arrived(block, half)
             spread_last(block, half)
 
-    for b in range(PACK):
-        bins = slice(b * QUADS, (b + 1) * QUADS)
-        fc, fs = far_cos[:, bins].T, far_sin[:, bins].T
-        nc, ns = near_cos[bins, :], near_sin[bins, :]
-        for a in range(LAGS // 128):
-            columns = slice(a * 128, (a + 1) * 128)
-            ca, sa = fc[:, a : a + 1], fs[:, a : a + 1]
-            inverse[2 * b * QUADS : (2 * b + 1) * QUADS, columns] = (ca * nc - sa * ns).astype(bf16)
-            inverse[(2 * b + 1) * QUADS : (2 * b + 2) * QUADS, columns] = -(sa * nc + ca * ns).astype(bf16)
-    inverse_out = pltpu.make_async_copy(inverse, inverse_hbm, out_sem.at[0])
-    inverse_out.start()
+    ca, sa, cb, sb = row_cos[1:2, :], row_sin[1:2, :], step_cos[...], step_sin[...]
+    near_cos[...] = jnp.concatenate([cb, ca * cb - sa * sb], axis=0).T
+    near_sin[...] = jnp.concatenate([sb, sa * cb + ca * sb], axis=0).T
+    lags = [128 // STEP * a - LAGS // 2 // STEP for a in range(LAGS // 128)]
+    angles = [row_cos[abs(a) : abs(a) + 1, :] for a in lags]
+    angles += [row_sin[abs(a) : abs(a) + 1, :] * (1.0 if a >= 0 else -1.0) for a in lags]
+    far[...] = jnp.concatenate(angles + [jnp.zeros((128 - len(angles), F), f32)], axis=0).T
+    for b in range(PAIR):
+        for h in range(2):
+            bins = pl.ds(2 * b + h, QUADS, stride=PACK)
+            nc, ns, fc = near_cos[bins, :], near_sin[bins, :], far[bins, :]
+            k = (h * 4 + b * 2) * QUADS
+            for a in range(LAGS // 128):
+                columns = slice(a * 128, (a + 1) * 128)
+                ca, sa = fc[:, a : a + 1], fc[:, len(lags) + a : len(lags) + a + 1]
+                inverse[k : k + QUADS, columns] = (ca * nc - sa * ns).astype(bf16)
+                inverse[k + QUADS : k + 2 * QUADS, columns] = (-sa * nc - ca * ns).astype(bf16)
+    inverse_copy = pltpu.make_async_copy(inverse, inverse_out, out_sem.at[0])
+    inverse_copy.start()
 
     def far_pass(i):
         yy, xx, zz = walk(i)
@@ -439,6 +455,21 @@
             cross(block, half)
 
     loop(0, NY * NZ, far_last)
+
+    def stacked_copy(first, count):
+        where = pl.ds(pl.multiple_of(first, 8 * C), count)
+        return pltpu.make_async_copy(stacked.at[where], stacked_out.at[where], out_sem.at[1])
+
+    def turn_sources(i):
+        for u in range(8):
+            where = pl.ds(pl.multiple_of((i * 8 + u) * C, C), C)
+            for h in range(2):
+                flipped = crossed[h, pl.ds(i * 8 + u, QUADS, stride=S), :].T.astype(bf16)
+                for k in range(4):
+                    stacked[where, (h * 4 + k) * 128 : (h * 4 + k + 1) * 128] = flipped[k * 32 : (k + 1) * 32]
+        stacked_copy(i * 8 * C, 8 * C).start()
+
+    loop(0, S // 8, turn_sources)
 
     def finish_win(k):
         trade(k).wait_send()
@@ -490,27 +521,8 @@
                 sent(far_block(half, 1, along, 1), half, 4)
 
     loop(0, NY * NZ, sent_far)
-    inverse_out.wait()
-    result_out(0, QUADS * S).wait()
-
-
-def to_lags(scaling, crossed, inverse, out, even, odd):
-    def both(fill, full):
-        out[...] = (mxu(full[...], inverse[...]) * scaling).reshape(8, C, LAGS)
-        for s in range(8):
-            for h in range(2):
-                flipped = crossed[h, :, s, :].T.astype(bf16)
-                for k in range(4):
-                    columns = slice((h * 4 + k) * 128, (h * 4 + k + 1) * 128)
-                    fill[s * C : (s + 1) * C, columns] = flipped[k * 32 : (k + 1) * 32]
-
-    @pl.when(lax.rem(pl.program_id(0), 2) == 0)
-    def _():
-        both(even, odd)
-
-    @pl.when(lax.rem(pl.program_id(0), 2) == 1)
-    def _():
-        both(odd, even)
+    inverse_copy.wait()
+    stacked_copy(0, S * C).wait()
 
 
 def turn(bins, steps):
@@ -518,15 +530,11 @@
     return jnp.cos(phase), jnp.sin(phase)
 
 
-def forward_parts():
-    bins = (K0 + jnp.arange(F, dtype=i32))[None, :]
-    return turn(bins, STEP * jnp.arange(L // STEP, dtype=i32)[:, None]) + turn(bins, jnp.arange(STEP, dtype=i32)[:, None])
-
-
-def inverse_parts():
-    bins = (K0 + PACK * jnp.arange(QUADS, dtype=i32)[None, :] + jnp.arange(PACK, dtype=i32)[:, None]).reshape(F)
-    far = turn(bins[None, :], 128 * jnp.arange(LAGS // 128, dtype=i32)[:, None] - LAGS // 2)
-    return far + turn(bins[:, None], jnp.arange(128, dtype=i32)[None, :])
+def angle_parts():
+    count = jnp.arange(40, dtype=i32)
+    scale = jnp.where(count < 16, 8 * STEP, jnp.where(count < 24, STEP, jnp.where(count < 32, 8, 1)))
+    steps = jnp.where(count < 16, count, count % 8) * scale
+    return turn((K0 + jnp.arange(F, dtype=i32))[None, :], steps[:, None])
 
 
 def per_device(traces, filter_taps, good_channels, source_index):
@@ -534,15 +542,24 @@
     smem = pl.BlockSpec(memory_space=pltpu.SMEM)
     anywhere = pl.BlockSpec(memory_space=pl.ANY)
     dma = pltpu.SemaphoreType.DMA
-    crossed, inverse = pl.pallas_call(
+    stacked, inverse = pl.pallas_call(
         whole,
         out_shape=(
-            jax.ShapeDtypeStruct((2, QUADS * S, 128), f32),
+            jax.ShapeDtypeStruct((S * C, 2 * F), bf16),
             jax.ShapeDtypeStruct((2 * F, LAGS), bf16),
         ),
-        in_specs=[anywhere] + [vmem] * 11,
+        in_specs=[anywhere] + [vmem] * 5,
         out_specs=(anywhere, anywhere),
         scratch_shapes=[
+            pltpu.VMEM((L // STEP, F), f32),
+            pltpu.VMEM((L // STEP, F), f32),
+            pltpu.VMEM((STEP, F), f32),
+            pltpu.VMEM((STEP, F), f32),
+            pltpu.VMEM((F, 128), f32),
+            pltpu.VMEM((F, 128), f32),
+            pltpu.VMEM((F, 128), f32),
+            pltpu.VMEM((PAIR, 256, 1024), bf16),
+            pltpu.VMEM((S * C, 2 * F), bf16),
             pltpu.VMEM((W * C, L), bf16),
             pltpu.VMEM((L, 256), bf16),
             pltpu.VMEM((F // 128, W, C, 256), f32),
@@ -566,27 +583,16 @@
             dma((BLK, 2, 5)), dma((BLK, 2)), dma((3,)),
         ],
         compiler_params=pltpu.CompilerParams(
-            collective_id=0, has_side_effects=True, vmem_limit_bytes=60 << 20
+            collective_id=0, has_side_effects=True, vmem_limit_bytes=LIMIT << 20
         ),
         name="whole",
     )(
         traces.reshape(W * C, L), good_channels.astype(i32)[None, :], filter_taps[None, :],
-        source_index.astype(i32)[None, :], *forward_parts(), *inverse_parts(),
+        source_index.astype(i32)[None, :], *angle_parts(),
     )
 
-    return pl.pallas_call(
-        functools.partial(to_lags, 1.0 / math.sqrt(F * W * WIN)),
-        grid=(S // 8 + 1,),
-        out_shape=jax.ShapeDtypeStruct((S, C, LAGS), f32),
-        in_specs=[
-            pl.BlockSpec((2, QUADS, 8, 128), lambda i: (0, 0, jnp.minimum(i, S // 8 - 1), 0)),
-            pl.BlockSpec((2 * F, LAGS), lambda i: (0, 0), pipeline_mode=pl.Buffered(1)),
-        ],
-        out_specs=pl.BlockSpec((8, C, LAGS), lambda i: (jnp.maximum(i - 1, 0), 0, 0)),
-        scratch_shapes=[pltpu.VMEM((8 * C, 2 * F), bf16)] * 2,
-        compiler_params=pltpu.CompilerParams(vmem_limit_bytes=62 << 20),
-        name="to_lags",
-    )(crossed.reshape(2, QUADS, S, 128), inverse)
+    scaling = 1.0 / math.sqrt(F * W * WIN)
+    return (mxu(stacked, inverse) * scaling).reshape(S, C, LAGS)
 
 
 def solution(mesh):

time: 115 us -> 103 us (0.90)
  Pallas kernels: 109 us -> 86.1 us
  matrix products: 0 us -> 15.5 us
  other arithmetic: 5.95 us -> 1.09 us
    pallas_call x2 -> x1, Pallas kernels: 109 us -> 86.1 us  [per_device(): pl.pallas_call(whole, out_shape=(jax.ShapeDtypeStruct((S * C, 2 * F), bf1...]
    dot_general x0 -> x1, matrix products: none -> 15.5 us  [mxu(): return jnp.dot(a, b, preferred_element_type=f32)]
    sin x4 -> x1, other arithmetic: 5.93 us -> 1.08 us  [turn(): return (jnp.cos(phase), jnp.sin(phase))]
where the time goes in v5:
time: 103 us
  Pallas kernels  86.1 us (84%)
  matrix products  15.5 us (15%)
  other arithmetic  1.09 us (1%)
    pallas_call x1, Pallas kernels, per_device(): pl.pallas_call(whole, out_shape=(jax.ShapeDtypeStruct((S * C, 2 * F), bf1...  86.1 us
    dot_general x1, matrix products, mxu(): return jnp.dot(a, b, preferred_element_type=f32)  15.5 us

profile of v5, /device:TPU:4, one launch (start us, length us, event | category | flops | bytes accessed | tf_op | source)
XLA Modules:
  0.0 102.7 jit_solution(8810526835799461270)
XLA Ops:
  0.0 1.1 %fusion.4 = (f32[40,512]{1,0:T(8,128)}, f32[40,512]{1,0:T(8,128)}) fusion(s32[40]{0:T(128)S(1)} %fusion.7, s32[512]{0:T(512)S(1)} %iota_add_fusion), kind=kLoop, calls=%fused_computation.7 | loop fusion | flops 184320 | bytes 166048 | tf_op jit(solution)/shard_map/sin | solution.py:530
  1.1 86.1 %whole.1 = (bf16[2048,1024]{1,0:T(8,128)(2,1)}, bf16[1024,2048]{1,0:T(8,128)(2,1)}) custom-call(bf16[256,7680]{1,0:T(8,128)(2,1)} %bitcast.7, s32[1,32]{1,0:T(1,128)} %bitcast.9, bf16[1,32]{1,0:T(2,128)(2,1)} %bitcast.10, s32[1,256]{1,0:T(1,128)} %bitcast.8, f32[40,512]{1,0:T(8,128)} %get-tuple-element.10.cosines, f32[40,512]{1,0:T(8,128)} %get-tuple-element.9.sines), custom_call_target="tpu_custom_call" | custom-call | tf_op jit(solution)/shard_map/whole/pallas_call | solution.py:545
  87.2 15.5 %convolution_multiply_fusion = f32[2048,2048]{1,0:T(8,128)} fusion(bf16[2048,1024]{1,0:T(8,128)(2,1)} %get-tuple-element.7, bf16[1024,2048]{1,0:T(8,128)(2,1)} %get-tuple-element.8), kind=kOutput, calls=%fused_computation | convolution fusion | flops 8594128896 | bytes 25165824 | tf_op jit(solution)/shard_map/dot_general | solution.py:41
  (2 shorter events, 0.0 us)

commit v6 on v5

--- a/solution.py
+++ b/solution.py
@@ -1,3 +1,4 @@
+import functools
 import math
 
 import jax
@@ -27,6 +28,7 @@
 PACK = 4
 PAIR = 2
 LIMIT = 54
+AT_ONCE = 16
 STEP = 64
 DEEP = 2 * W * WIN
 MESH = pl.DeviceIdType.MESH
@@ -353,12 +355,12 @@
     for q in range(2 * per_half):
         held[me, q] = quads[q]
 
-    loop(0, 2 * tiles, lambda t: to_group(2, t, diagonal_group, sibling).wait_recv())
-    turn_group(diagonal_group)
-
     for half in (0, 1):
         arrived(z_over, half)
         spread(z_over, half)
+
+    loop(0, 2 * tiles, lambda t: to_group(2, t, diagonal_group, sibling).wait_recv())
+    turn_group(diagonal_group)
 
     def widen(i):
         start = pl.multiple_of(i * 512, 512)
@@ -523,6 +525,10 @@
     loop(0, NY * NZ, sent_far)
     inverse_copy.wait()
     stacked_copy(0, S * C).wait()
+
+
+def to_lags(scaling, stacked, inverse, out):
+    out[...] = (mxu(stacked[...], inverse[...]) * scaling).reshape(out.shape)
 
 
 def turn(bins, steps):
@@ -592,7 +598,18 @@
     )
 
     scaling = 1.0 / math.sqrt(F * W * WIN)
-    return (mxu(stacked, inverse) * scaling).reshape(S, C, LAGS)
+    return pl.pallas_call(
+        functools.partial(to_lags, scaling),
+        grid=(S // AT_ONCE,),
+        out_shape=jax.ShapeDtypeStruct((S, C, LAGS), f32),
+        in_specs=[
+            pl.BlockSpec((AT_ONCE * C, 2 * F), lambda i: (i, 0)),
+            pl.BlockSpec((2 * F, LAGS), lambda i: (0, 0), pipeline_mode=pl.Buffered(1)),
+        ],
+        out_specs=pl.BlockSpec((AT_ONCE, C, LAGS), lambda i: (i, 0, 0)),
+        compiler_params=pltpu.CompilerParams(vmem_limit_bytes=62 << 20),
+        name="to_lags",
+    )(stacked, inverse)
 
 
 def solution(mesh):

time: 103 us -> 102 us (level)
  matrix products: 15.5 us -> 0 us
  Pallas kernels: 86.1 us -> 101 us
    dot_general x1 -> x0, matrix products: 15.5 us -> none  [mxu(): return jnp.dot(a, b, preferred_element_type=f32)]
    pallas_call x0 -> x1, Pallas kernels: none -> 13.9 us  [per_device(): pl.pallas_call(functools.partial(to_lags, scaling), grid=(S // AT_ONCE,),...]
where the time goes in v6:
time: 102 us
  Pallas kernels  101 us (99%)
  other arithmetic  1.09 us (1%)
    pallas_call x1, Pallas kernels, per_device(): pl.pallas_call(whole, out_shape=(jax.ShapeDtypeStruct((S * C, 2 * F), bf1...  86.6 us
    pallas_call x1, Pallas kernels, per_device(): pl.pallas_call(functools.partial(to_lags, scaling), grid=(S // AT_ONCE,),...  13.9 us

profile of v6, /device:TPU:4, one launch (start us, length us, event | category | flops | bytes accessed | tf_op | source)
XLA Modules:
  0.0 101.6 jit_solution(1997911630462646511)
XLA Ops:
  0.0 1.1 %fusion.4 = (f32[40,512]{1,0:T(8,128)}, f32[40,512]{1,0:T(8,128)}) fusion(s32[40]{0:T(128)S(1)} %fusion.7, s32[512]{0:T(512)S(1)} %iota_add_fusion), kind=kLoop, calls=%fused_computation.6 | loop fusion | flops 184320 | bytes 166048 | tf_op jit(solution)/shard_map/sin | solution.py:536
  1.1 86.6 %whole.1 = (bf16[2048,1024]{1,0:T(8,128)(2,1)}, bf16[1024,2048]{1,0:T(8,128)(2,1)}) custom-call(bf16[256,7680]{1,0:T(8,128)(2,1)} %bitcast.4, s32[1,32]{1,0:T(1,128)} %bitcast.6, bf16[1,32]{1,0:T(2,128)(2,1)} %bitcast.7, s32[1,256]{1,0:T(1,128)} %bitcast.5, f32[40,512]{1,0:T(8,128)} %get-tuple-element.10.cosines, f32[40,512]{1,0:T(8,128)} %get-tuple-element.9.sines), custom_call_target="tpu_custom_call" | custom-call | tf_op jit(solution)/shard_map/whole/pallas_call | solution.py:551
  87.7 13.9 %to_lags.1 = f32[64,32,2048]{2,1,0:T(8,128)} custom-call(bf16[2048,1024]{1,0:T(8,128)(2,1)} %get-tuple-element.7.stacked, bf16[1024,2048]{1,0:T(8,128)(2,1)} %get-tuple-element.8.inverse), custom_call_target="tpu_custom_call" | custom-call | tf_op jit(solution)/shard_map/to_lags/pallas_call | solution.py:601
  (2 shorter events, 0.0 us)

commit v7 on v6

--- a/solution.py
+++ b/solution.py
@@ -355,58 +355,6 @@
     for q in range(2 * per_half):
         held[me, q] = quads[q]
 
-    for half in (0, 1):
-        arrived(z_over, half)
-        spread(z_over, half)
-
-    loop(0, 2 * tiles, lambda t: to_group(2, t, diagonal_group, sibling).wait_recv())
-    turn_group(diagonal_group)
-
-    def widen(i):
-        start = pl.multiple_of(i * 512, 512)
-        real, imag = turned[pl.ds(start, 512), :], turned[pl.ds(F * 8 + start, 512), :]
-        both = jnp.concatenate([real, imag], axis=1).reshape(16, 2, 16, 256)
-        for b in range(PAIR):
-            spread_rows = mxu(both[:, b].reshape(256, 256).astype(bf16), spread_pair[b])
-            for p in range(4):
-                upper = spread_rows[:, p * 256 : p * 256 + 128].reshape(32, 8, 128)
-                lower = spread_rows[:, p * 256 + 128 : p * 256 + 256].reshape(32, 8, 128)
-                tile = jnp.concatenate([upper, lower], axis=1).astype(bf16)
-                wide[pl.ds(pl.multiple_of(i * 32, 32), 32), p * 32 + b * 16 : p * 32 + b * 16 + 16, :] = tile
-
-    loop(0, F * 8 // 512, widen)
-
-    def cross(block, half):
-        for j in range(per_half):
-            quad = place(block) * (2 * per_half) + half * per_half + j
-            rows = pl.ds(pl.multiple_of(quad * S, S), S)
-            for h in range(2):
-                crossed[h, rows, :] = mxu(held[block, half * per_half + j, :, h * 128 : (h + 1) * 128], wide[quad * 2 + h])
-
-    def near_block(half, step, zz):
-        return at(y + step, zz, x) if half == 0 else at(y, zz, x + step)
-
-    def far_block(half, step, along, zz):
-        return at(along, zz, x + step) if half == 0 else at(y + step, zz, along)
-
-    for zz in (z, z + 1):
-        for half in (0, 1):
-            for step in (-1, 1):
-                block = near_block(half, step, zz)
-                arrived(block, half)
-
-                @pl.when(lax.rem(zz, NZ) == (0 if step == -1 else 1))
-                def _():
-                    hop(block, half, 1 if step == -1 else 2, first[half][0 if step == -1 else 1]).start()
-
-                spread_last(block, half)
-
-    for zz in (0, 1):
-        for half in (0, 1):
-            block = near_block(half, 2, zz)
-            arrived(block, half)
-            spread_last(block, half)
-
     ca, sa, cb, sb = row_cos[1:2, :], row_sin[1:2, :], step_cos[...], step_sin[...]
     near_cos[...] = jnp.concatenate([cb, ca * cb - sa * sb], axis=0).T
     near_sin[...] = jnp.concatenate([sb, sa * cb + ca * sb], axis=0).T
@@ -426,6 +374,58 @@
                 inverse[k + QUADS : k + 2 * QUADS, columns] = (-sa * nc - ca * ns).astype(bf16)
     inverse_copy = pltpu.make_async_copy(inverse, inverse_out, out_sem.at[0])
     inverse_copy.start()
+
+    for half in (0, 1):
+        arrived(z_over, half)
+        spread(z_over, half)
+
+    loop(0, 2 * tiles, lambda t: to_group(2, t, diagonal_group, sibling).wait_recv())
+    turn_group(diagonal_group)
+
+    def widen(i):
+        start = pl.multiple_of(i * 512, 512)
+        real, imag = turned[pl.ds(start, 512), :], turned[pl.ds(F * 8 + start, 512), :]
+        both = jnp.concatenate([real, imag], axis=1).reshape(16, 2, 16, 256)
+        for b in range(PAIR):
+            spread_rows = mxu(both[:, b].reshape(256, 256).astype(bf16), spread_pair[b])
+            for p in range(4):
+                upper = spread_rows[:, p * 256 : p * 256 + 128].reshape(32, 8, 128)
+                lower = spread_rows[:, p * 256 + 128 : p * 256 + 256].reshape(32, 8, 128)
+                tile = jnp.concatenate([upper, lower], axis=1).astype(bf16)
+                wide[pl.ds(pl.multiple_of(i * 32, 32), 32), p * 32 + b * 16 : p * 32 + b * 16 + 16, :] = tile
+
+    loop(0, F * 8 // 512, widen)
+
+    def cross(block, half):
+        for j in range(per_half):
+            quad = place(block) * (2 * per_half) + half * per_half + j
+            rows = pl.ds(pl.multiple_of(quad * S, S), S)
+            for h in range(2):
+                crossed[h, rows, :] = mxu(held[block, half * per_half + j, :, h * 128 : (h + 1) * 128], wide[quad * 2 + h])
+
+    def near_block(half, step, zz):
+        return at(y + step, zz, x) if half == 0 else at(y, zz, x + step)
+
+    def far_block(half, step, along, zz):
+        return at(along, zz, x + step) if half == 0 else at(y + step, zz, along)
+
+    for zz in (z, z + 1):
+        for half in (0, 1):
+            for step in (-1, 1):
+                block = near_block(half, step, zz)
+                arrived(block, half)
+
+                @pl.when(lax.rem(zz, NZ) == (0 if step == -1 else 1))
+                def _():
+                    hop(block, half, 1 if step == -1 else 2, first[half][0 if step == -1 else 1]).start()
+
+                spread_last(block, half)
+
+    for zz in (0, 1):
+        for half in (0, 1):
+            block = near_block(half, 2, zz)
+            arrived(block, half)
+            spread_last(block, half)
 
     def far_pass(i):
         yy, xx, zz = walk(i)

time: 102 us -> 98.1 us (0.962)
  Pallas kernels: 101 us -> 96.7 us
    pallas_call x1, Pallas kernels: 86.6 us -> 82.7 us  [per_device(): pl.pallas_call(whole, out_shape=(jax.ShapeDtypeStruct((S * C, 2 * F), bf1...]
where the time goes in v7:
time: 98.1 us; the launch traced here: 97.8 us
  Pallas kernels  96.7 us (99%)
  other arithmetic  1.09 us (1%)
    pallas_call x1, Pallas kernels, per_device(): pl.pallas_call(whole, out_shape=(jax.ShapeDtypeStruct((S * C, 2 * F), bf1...  82.7 us
    pallas_call x1, Pallas kernels, per_device(): pl.pallas_call(functools.partial(to_lags, scaling), grid=(S // AT_ONCE,),...  13.9 us

profile of v7, /device:TPU:4, one launch (start us, length us, event | category | flops | bytes accessed | tf_op | source)
XLA Modules:
  0.0 97.8 jit_solution(14194591567901724350)
XLA Ops:
  0.0 1.1 %fusion.4 = (f32[40,512]{1,0:T(8,128)}, f32[40,512]{1,0:T(8,128)}) fusion(s32[40]{0:T(128)S(1)} %fusion.7, s32[512]{0:T(512)S(1)} %iota_add_fusion), kind=kLoop, calls=%fused_computation.6 | loop fusion | flops 184320 | bytes 166048 | tf_op jit(solution)/shard_map/sin | solution.py:536
  1.1 82.7 %whole.1 = (bf16[2048,1024]{1,0:T(8,128)(2,1)}, bf16[1024,2048]{1,0:T(8,128)(2,1)}) custom-call(bf16[256,7680]{1,0:T(8,128)(2,1)} %bitcast.4, s32[1,32]{1,0:T(1,128)} %bitcast.6, bf16[1,32]{1,0:T(2,128)(2,1)} %bitcast.7, s32[1,256]{1,0:T(1,128)} %bitcast.5, f32[40,512]{1,0:T(8,128)} %get-tuple-element.10.cosines, f32[40,512]{1,0:T(8,128)} %get-tuple-element.9.sines), custom_call_target="tpu_custom_call" | custom-call | tf_op jit(solution)/shard_map/whole/pallas_call | solution.py:551
  83.8 13.9 %to_lags.1 = f32[64,32,2048]{2,1,0:T(8,128)} custom-call(bf16[2048,1024]{1,0:T(8,128)(2,1)} %get-tuple-element.7.stacked, bf16[1024,2048]{1,0:T(8,128)(2,1)} %get-tuple-element.8.inverse), custom_call_target="tpu_custom_call" | custom-call | tf_op jit(solution)/shard_map/to_lags/pallas_call | solution.py:601
  (2 shorter events, 0.0 us)
